TPU v7x, 512 devices: a whole 4x8x8 slice. The times are simulated.
512 devices in a mesh: space: 64 (over x, y, z_lo), dp: 8 (over z_hi, core).
Axes of the slice: x: 4, y: 8, z: 8 (z_hi: 4, z_lo: 2; z = z_hi * 2 + z_lo), core: 2. Of those that a mesh axis runs over, the one named last changes fastest.
Arguments:
- volumes: bfloat16 [8, 4, 256, 32, 32], P('dp', None, 'space'), may hold values from -6 to 6
- kernel_one: bfloat16 [32, 4, 3, 3, 3], replicated, may hold values from -0.625 to 0.625
- kernel_two: bfloat16 [64, 32, 3, 3, 3], replicated, may hold values from -0.21875 to 0.21875
- cotangent: bfloat16 [8, 64, 128, 256], P('dp', None, 'space'), may hold values from -6 to 6
Outputs:
- features: bfloat16 [8, 64, 128, 256], P('dp', None, 'space')
- pooled_grad: bfloat16 [8, 32, 128, 256], P('dp', None, 'space')
- grad_one: float32 [3456], P('space')
- grad_two: float32 [55296], P('space')
All inputs are finite; a program needn't handle non-finite values.
Results may differ from a plain program's by a relative error of at most 0.006.
Values may be sent and summed in bfloat16 or wider, within the bound.
A program may use at most 64 MiB of HBM per device.

v0:
```python
import math

import jax
import jax.numpy as jnp
from jax import lax
from jax.sharding import PartitionSpec as P


def extended_2(block, sides, width):
    for axis, dim in sides:
        count = lax.axis_size(axis)
        forward = [(i, i + 1) for i in range(count - 1)]
        backward = [(target, source) for source, target in forward]
        low = lax.ppermute(
            lax.slice_in_dim(block, block.shape[dim] - width, None, axis=dim), axis, forward
        )
        high = lax.ppermute(lax.slice_in_dim(block, 0, width, axis=dim), axis, backward)
        block = jnp.concatenate([low, block, high], axis=dim)
    return block


def silu(v):
    return v * jax.nn.sigmoid(v)


def dsilu(v):
    s = jax.nn.sigmoid(v)
    return s * (1.0 + v * (1.0 - s))


def conv_local(inputs, kernel):
    return lax.conv_general_dilated(
        inputs,
        kernel,
        (1, 1, 1),
        [(0, 0), (1, 1), (1, 1)],
        dimension_numbers=("NCDHW", "OIDHW", "NCDHW"),
        preferred_element_type=jnp.float32,
    )


def kernel_term(padded, delta):
    left = jnp.swapaxes(padded, 0, 1)
    right = jnp.swapaxes(delta, 0, 1)
    result = lax.conv_general_dilated(
        left,
        right,
        (1, 1, 1),
        [(0, 0), (1, 1), (1, 1)],
        dimension_numbers=("NCDHW", "OIDHW", "NCDHW"),
        preferred_element_type=jnp.float32,
    )
    return jnp.transpose(result, (1, 0, 2, 3, 4))


def pool_block(field):
    batch, chans, depth, rows, cols = field.shape
    return field.reshape(batch, chans, depth // 2, 2, rows // 2, 2, cols // 2, 2).mean(
        axis=(3, 5, 7)
    )


def pooled_planes(extended, kernel_one, count):

    def one_plane(index):
        window = lax.dynamic_slice_in_dim(extended, 2 * index, 4, 2)
        pre_block = conv_local(window, kernel_one)
        return (pool_block(silu(pre_block)).astype(jnp.bfloat16), pre_block)

    stacked, pre_stack = lax.map(one_plane, jnp.arange(count, dtype=jnp.int32))
    return (jnp.moveaxis(stacked[:, 0, :, 0], 0, 1)[None], pre_stack)


def on_device(volumes, kernel_one, kernel_two, cotangent):
    planes = volumes.shape[2]
    blocks = planes // 2
    width = volumes.shape[3]
    half = width // 2
    slabs = lax.axis_size("space")
    cot_cells = cotangent.reshape(
        cotangent.shape[0], cotangent.shape[1], cotangent.shape[2], half, half
    )
    extended = extended_2(volumes, (("space", 2),), 1)
    pooled, pre_stack = pooled_planes(extended, kernel_one, blocks)
    pooled_ext = extended_2(pooled, (("space", 2),), 1)
    pre_two = conv_local(pooled_ext, kernel_two)
    features = silu(pre_two).astype(jnp.bfloat16)
    delta_two = (cot_cells.astype(jnp.float32) * dsilu(pre_two)).astype(jnp.bfloat16)
    flipped = jnp.transpose(jnp.flip(kernel_two, (2, 3, 4)), (1, 0, 2, 3, 4))
    delta_ext = extended_2(delta_two, (("space", 2),), 1)
    pooled_grad = conv_local(delta_ext, flipped).astype(jnp.bfloat16)
    term_two = kernel_term(pooled_ext, delta_two)

    def block_step(index, total):
        window = lax.dynamic_slice_in_dim(extended, 2 * index, 4, 2)
        pre_one = lax.dynamic_index_in_dim(pre_stack, index, 0, keepdims=False)
        plane = lax.dynamic_slice_in_dim(pooled_grad, index, 1, 2).astype(jnp.float32) * 0.125
        spread = jnp.repeat(jnp.repeat(jnp.repeat(plane, 2, axis=2), 2, axis=3), 2, axis=4)
        delta_one = (spread * dsilu(pre_one)).astype(jnp.bfloat16)
        return total + kernel_term(window, delta_one)

    term_one = lax.fori_loop(0, blocks, block_step, jnp.zeros(kernel_one.shape, jnp.float32))
    count = lax.axis_size("dp") * planes * slabs * width * width
    flat_one = term_one.reshape(-1) * (1.0 / math.sqrt(count))
    flat_two = term_two.reshape(-1) * (1.0 / math.sqrt(count // 8))
    total_one, total_two = lax.psum((flat_one, flat_two), ("space", "dp"))
    where_me = lax.axis_index("space")
    piece_one = total_one.shape[0] // slabs
    piece_two = total_two.shape[0] // slabs
    grad_one = lax.dynamic_slice_in_dim(total_one, where_me * piece_one, piece_one, 0)
    grad_two = lax.dynamic_slice_in_dim(total_two, where_me * piece_two, piece_two, 0)
    features_flat = features.reshape(
        features.shape[0], features.shape[1], features.shape[2], half * half
    )
    pooled_grad_flat = pooled_grad.reshape(
        pooled_grad.shape[0], pooled_grad.shape[1], pooled_grad.shape[2], half * half
    )
    return (features_flat, pooled_grad_flat, grad_one, grad_two)


def solution(mesh):
    in_specs = (P("dp", None, "space", None, None), P(), P(), P("dp", None, "space", None))
    out_specs = (P("dp", None, "space", None), P("dp", None, "space", None), P("space"), P("space"))
    return jax.shard_map(
        on_device, mesh=mesh, in_specs=in_specs, out_specs=out_specs, check_vma=False
    )
```

profile of v0, /device:TPU:1, one launch (start us, length us, event | category | flops | bytes accessed | tf_op | source)
XLA Modules:
  0.0 371.0 jit_solution(14522617791158183917)
XLA Ops:
  7.2 0.8 fusion.52
  8.1 4.8 %collective-permute-start = (bf16[1,4,1,32,32]{4,3,2,1,0:T(8,128)(2,1)S(1)}, bf16[1,4,1,32,32]{4,3,2,1,0:T(8,128)(2,1)S(1)}, u32[]{:S(2)}, u32[]{:S(2)}) collective-permute-start(bf16[1,4,1,32,32]{4,3,2,1,0:T(8,128)(2,1)S(1)} %get-tuple-element.301), channel_id=1, source_target_pairs={{0,8},{8,16},{16,24},{24,32},{32,40},{40,48},{48,56},{56,64},{64,7... | collective-permute-start | bytes 24584 | tf_op jit(solution)/shard_map/ppermute | solution.py:14
  12.9 1.3 collective-permute-start.1
  14.2 0.6 constant_dynamic-update-slice_fusion.2
  14.8 1.6 constant_dynamic-update-slice_fusion.1
  16.4 1.1 collective-permute-done.1
  18.1 21.0 %while.26 = (s32[]{:T(128)}, bf16[2,1,32,1,16,16]{2,4,5,3,1,0:T(8,128)(2,1)S(1)}, f32[2,1,32,2,32,32]{2,4,5,3,1,0:T(8,128)}, s32[2]{0:T(128)S(1)}, bf16[1,4,6,32...) while((s32[]{:T(128)}, ...), condition=%wide.region_3.4_spmd, body=%wide.region_0.3_spmd.sunk | while | flops 17981444 | bytes 9416969 | solution.py:70
  19.4 0.9 constant_dynamic-slice_fusion.4
  20.5 0.9 copy.239
  21.7 3.1 divide_multiply_fusion.2
  25.9 1.3 copy-done.1
  27.3 1.3 copy-done.2
  29.9 0.9 constant_dynamic-slice_fusion.4
  31.0 0.9 copy.239
  32.1 3.1 divide_multiply_fusion.2
  36.4 1.3 copy-done.1
  37.8 1.3 copy-done.2
  39.1 3.2 collective-permute-start.2
  42.4 1.3 collective-permute-start.3
  43.8 3.5 collective-permute-done.3
  47.7 1.0 add_multiply_fusion
  48.9 4.1 %collective-permute-start.4 = (bf16[1,64,1,16,16]{1,4,3,2,0:T(8,128)(2,1)S(1)}, bf16[1,64,1,16,16]{1,4,3,2,0:T(8,128)(2,1)S(1)}, u32[]{:S(2)}, u32[]{:S(2)}) collective-permute-start(bf16[1,64,1,16,16]{1,4,3,2,0:T(8,128)(2,1)S(1)} %get-tuple-element.296), channel_id=1, source_target_pairs={{0,8},{8,16},{16,24},{24,32},{32,40},{40,48},{48,56},{56,64},{64,7... | collective-permute-start | bytes 98312 | tf_op jit(solution)/shard_map/ppermute | solution.py:14
  53.0 1.5 collective-permute-start.5
  54.6 3.1 convolution_multiply_fusion
  57.7 0.7 copy.212
  58.5 12.2 %copy.211 = f32[64,32,3,3,3]{4,3,2,1,0:T(4,128)} copy(f32[64,32,3,3,3]{0,1,4,3,2:T(8,128)S(1)} %convolution_multiply_fusion) | data formatting | bytes 442368 | tf_op jit(solution)/shard_map/mul | solution.py:105
  70.6 11.0 %mul.119 = f32[55296]{0:T(1024)} reshape(f32[64,32,3,3,3]{4,3,2,1,0:T(4,128)} %copy.211) | data formatting | bytes 442368 | tf_op jit(solution)/shard_map/mul | solution.py:105
  82.1 1.5 fusion.23
  83.6 0.7 copy.204
  84.3 40.6 %while.27 = (s32[]{:T(128)}, f32[32,4,3,3,3]{0,1,4,3,2:T(4,128)S(1)}, bf16[1,4,6,32,32]{4,3,2,1,0:T(8,128)(2,1)}, bf16[1,32,2,16,16]{1,4,3,2,0:T(8,128)(2,1)}, f...) while((s32[]{:T(128)}, ...), condition=%wide.region_5.6_spmd.clone, body=%wide.region_4.5_spmd.clone.sunk | while | flops 14185223 | bytes 2895017 | solution.py:102
  84.3 0.9 dynamic-slice_bitcast_fusion.2
  85.2 0.9 multiply_bitcast_fusion.2
  86.7 1.3 constant_dynamic-slice_fusion.5
  88.0 1.1 copy.243
  89.5 1.0 copy.246
  90.4 1.8 copy.242
  92.3 12.4 %convolution_add_fusion.2 = f32[32,4,3,3,3]{0,1,4,3,2:T(4,128)S(1)} fusion(bf16[4,1,4,32,32]{0,1,4,3,2:T(2,128)(2,1)S(1)} %copy.242, bf16[32,1,2,32,32]{0,1,4,3,2:T(2,128)(2,1)S(1)} %copy.246, f32[32,4,3,3,3]{0,1,4,3,2:T(4,128)S(1)} %get-tuple-element.423, pred[]{:T(512)S(6)} %compare.36), kind=kOutput, calls=%fused_computation.20.clone.1 | convolution fusion | flops 13579008 | bytes 191489 | tf_op jit(solution)/shard_map/while/body/eval_jaxpr/transpose | solution.py:53
  104.7 0.9 dynamic-slice_bitcast_fusion.2
  105.6 0.9 multiply_bitcast_fusion.2
  107.0 1.3 constant_dynamic-slice_fusion.5
  108.3 1.1 copy.243
  109.8 1.0 copy.246
  110.8 1.8 copy.242
  112.6 12.4 %convolution_add_fusion.2 = f32[32,4,3,3,3]{0,1,4,3,2:T(4,128)S(1)} fusion(bf16[4,1,4,32,32]{0,1,4,3,2:T(2,128)(2,1)S(1)} %copy.242, bf16[32,1,2,32,32]{0,1,4,3,2:T(2,128)(2,1)S(1)} %copy.246, f32[32,4,3,3,3]{0,1,4,3,2:T(4,128)S(1)} %get-tuple-element.423, pred[]{:T(512)S(6)} %compare.36), kind=kOutput, calls=%fused_computation.20.clone.1 | convolution fusion | flops 13579008 | bytes 191489 | tf_op jit(solution)/shard_map/while/body/eval_jaxpr/transpose | solution.py:53
  125.0 1.6 copy.213
  127.6 109.4 %psum.14 = f32[3456]{0:T(1024)S(1)} all-reduce(f32[3456]{0:T(1024)S(1)} %mul.115), channel_id=1, replica_groups=mesh['space'=64,'dp'=8] {'space','dp'}, use_global_device_ids=true, to_apply=%region_6.7 | all-reduce | flops 3456 | bytes 27648 | tf_op jit(solution)/shard_map/psum | solution.py:106
  237.6 125.2 %all-reduce.2.cloned.1.call-done = f32[55296]{0:T(1024)} async-done(((f32[55296]{0:T(1024)}), f32[55296]{0:T(1024)}) %all-reduce.2.cloned.1.call-update) | async-done | bytes 221200 | tf_op jit(solution)/shard_map/psum | solution.py:106
  362.7 1.4 dynamic_slice.36
  (83 shorter events, 9.7 us)
Async XLA Ops:
  7.2 40.5 %copy-start = (bf16[64,32,3,3,3]{0,1,4,3,2:T(8,128)(2,1)S(1)}, bf16[64,32,3,3,3]{0,1,4,3,2:T(8,128)(2,1)}, u32[]{:S(2)}) copy-start(bf16[64,32,3,3,3]{0,1,4,3,2:T(8,128)(2,1)} %param.10) | copy-start | bytes 331780
  7.2 355.6 %all-reduce.2.cloned.1.call-start = ((), (), s32[]{:S(2)}) async-start(), calls=%async_computation | async-start | bytes 442368 | tf_op jit(solution)/shard_map/psum | solution.py:106
  8.1 6.1 %collective-permute-start = (bf16[1,4,1,32,32]{4,3,2,1,0:T(8,128)(2,1)S(1)}, bf16[1,4,1,32,32]{4,3,2,1,0:T(8,128)(2,1)S(1)}, u32[]{:S(2)}, u32[]{:S(2)}) collective-permute-start(bf16[1,4,1,32,32]{4,3,2,1,0:T(8,128)(2,1)S(1)} %get-tuple-element.301), channel_id=1, source_target_pairs={{0,8},{8,16},{16,24},{24,32},{32,40},{40,48},{48,56},{56,64},{64,7... | collective-permute-start | bytes 24584 | tf_op jit(solution)/shard_map/ppermute | solution.py:14
  12.9 4.7 %collective-permute-start.1 = (bf16[1,4,1,32,32]{4,3,2,1,0:T(8,128)(2,1)S(1)}, bf16[1,4,1,32,32]{4,3,2,1,0:T(8,128)(2,1)S(1)}, u32[]{:S(2)}, u32[]{:S(2)}) collective-permute-start(bf16[1,4,1,32,32]{4,3,2,1,0:T(8,128)(2,1)S(1)} %get-tuple-element.300), channel_id=1, source_target_pairs={{8,0},{16,8},{24,16},{32,24},{40,32},{48,40},{56,48},{64,56},{72,6... | collective-permute-start | bytes 24584 | tf_op jit(solution)/shard_map/ppermute | solution.py:17
  18.1 25.5 %copy-start.3 = (bf16[1,64,2,256]{3,2,1,0:T(2,128)(2,1)S(1)}, bf16[1,64,2,256]{3,2,1,0:T(2,128)(2,1)}, u32[]{:S(2)}) copy-start(bf16[1,64,2,256]{3,2,1,0:T(2,128)(2,1)} %param.11) | copy-start | bytes 196612
  18.1 3.5 copy-start.4
  18.1 3.5 copy-start.5
  25.6 1.6 copy-start.1
  27.3 1.3 copy-start.2
  28.6 3.5 copy-start.4
  28.6 3.5 copy-start.5
  36.1 1.6 copy-start.1
  37.8 1.3 copy-start.2
  39.1 4.7 %collective-permute-start.2 = (bf16[1,32,1,16,16]{1,3,4,2,0:T(8,128)(2,1)S(1)}, bf16[1,32,1,16,16]{1,3,4,2,0:T(8,128)(2,1)S(1)}, u32[]{:S(2)}, u32[]{:S(2)}) collective-permute-start(bf16[1,32,1,16,16]{1,3,4,2,0:T(8,128)(2,1)S(1)} %get-tuple-element.298), channel_id=1, source_target_pairs={{0,8},{8,16},{16,24},{24,32},{32,40},{40,48},{48,56},{56,64},{64,7... | collective-permute-start | bytes 49160 | tf_op jit(solution)/shard_map/ppermute | solution.py:14
  42.4 5.0 %collective-permute-start.3 = (bf16[1,32,1,16,16]{1,3,4,2,0:T(8,128)(2,1)S(1)}, bf16[1,32,1,16,16]{1,3,4,2,0:T(8,128)(2,1)S(1)}, u32[]{:S(2)}, u32[]{:S(2)}) collective-permute-start(bf16[1,32,1,16,16]{1,3,4,2,0:T(8,128)(2,1)S(1)} %get-tuple-element.299), channel_id=1, source_target_pairs={{8,0},{16,8},{24,16},{32,24},{40,32},{48,40},{56,48},{64,56},{72,6... | collective-permute-start | bytes 49160 | tf_op jit(solution)/shard_map/ppermute | solution.py:17
  43.8 3.9 %copy-start.6 = (pred[8,3]{0,1:T(4,128)(4,1)S(1)}, pred[8,3]{0,1:T(4,128)(4,1)}, u32[]{:S(2)}) copy-start(pred[8,3]{0,1:T(4,128)(4,1)} %constant.108) | copy-start | bytes 76
  48.9 32.7 %collective-permute-start.4 = (bf16[1,64,1,16,16]{1,4,3,2,0:T(8,128)(2,1)S(1)}, bf16[1,64,1,16,16]{1,4,3,2,0:T(8,128)(2,1)S(1)}, u32[]{:S(2)}, u32[]{:S(2)}) collective-permute-start(bf16[1,64,1,16,16]{1,4,3,2,0:T(8,128)(2,1)S(1)} %get-tuple-element.296), channel_id=1, source_target_pairs={{0,8},{8,16},{16,24},{24,32},{32,40},{40,48},{48,56},{56,64},{64,7... | collective-permute-start | bytes 98312 | tf_op jit(solution)/shard_map/ppermute | solution.py:14
  53.0 28.6 %collective-permute-start.5 = (bf16[1,64,1,16,16]{1,4,3,2,0:T(8,128)(2,1)S(1)}, bf16[1,64,1,16,16]{1,4,3,2,0:T(8,128)(2,1)S(1)}, u32[]{:S(2)}, u32[]{:S(2)}) collective-permute-start(bf16[1,64,1,16,16]{1,4,3,2,0:T(8,128)(2,1)S(1)} %get-tuple-element.297), channel_id=1, source_target_pairs={{8,0},{16,8},{24,16},{32,24},{40,32},{48,40},{56,48},{64,56},{72,6... | collective-permute-start | bytes 98312 | tf_op jit(solution)/shard_map/ppermute | solution.py:17
Sparse Core Ops, SparseCore 0:
  81.8 280.9 all-reduce.1
where the time goes:
time: 372 us; the launch traced here: 371 us
  waiting for transfers between devices  130 us (35%)
  blocking collectives  109 us (29%)
  local copies, waits for them, and re-layouts  58.9 us (16%)
  matrix products  36.6 us (10%)
  starting transfers between devices  16.2 us (4%)
  between operations  14.4 us (4%)
  other arithmetic  3.91 us (1%)
    psum x1, waiting for transfers between devices, on_device(): total_one, total_two = lax.psum((flat_one, flat_two), ('space', 'dp'))  125 us
    psum x1, blocking collectives, on_device(): total_one, total_two = lax.psum((flat_one, flat_two), ('space', 'dp'))  109 us
    transpose x3, matrix products, kernel_term(): return jnp.transpose(result, (1, 0, 2, 3, 4))  27.8 us
    mul x2, local copies, waits for them, and re-layouts, on_device(): flat_two = term_two.reshape(-1) * (1.0 / math.sqrt(count // 8))  23.1 us
    ppermute x3, starting transfers between devices, extended_2(): lax.ppermute(lax.slice_in_dim(block, block.shape[dim] - width, None, axis...  12.1 us
    conv_general_dilated x4, matrix products, conv_local(): lax.conv_general_dilated(inputs, kernel, (1, 1, 1), [(0, 0), (1, 1), (1,...  8.74 us
  transfers between devices with their start and end apart: 7, of which 3 were waited for; matrix products, arithmetic and copies ran while one was open for 20% of the time, Pallas kernels for 0%

commit v1 on v0

v1 whole, which is shorter than its diff:
```python
import functools
import math

import jax
import jax.numpy as jnp
from jax import lax
from jax.experimental import pallas as pl
from jax.experimental.pallas import tpu as pltpu
from jax.sharding import PartitionSpec as P

F32 = jnp.float32
BF16 = jnp.bfloat16
TAPS = [(a, b) for a in (-1, 0, 1) for b in (-1, 0, 1)]
NT = (((1,), (1,)), ((), ()))


def dot(a, b):
    return jnp.dot(a, b, preferred_element_type=F32)


def dot_nt(a, b):
    return lax.dot_general(a, b, NT, preferred_element_type=F32)


def iota(shape, dim):
    return lax.broadcasted_iota(jnp.int32, shape, dim)


def tap_masks(width):
    lane = iota((1, width * width), 1)
    row, col = lane // width, lane % width
    rows = {-1: row >= 1, 0: None, 1: row < width - 1}
    cols = {-1: col >= 1, 0: None, 1: col < width - 1}
    masks = []
    for dr, dc in TAPS:
        parts = [m for m in (rows[dr], cols[dc]) if m is not None]
        mask = None
        for part in parts:
            mask = part if mask is None else jnp.logical_and(mask, part)
        masks.append(mask)
    return masks


def shifted(block, tap, masks, width, sign=1):
    dr, dc = TAPS[tap]
    dr, dc = sign * dr, sign * dc
    if dr == 0 and dc == 0:
        return block
    size = width * width
    moved = pltpu.roll(block, (-(dr * width + dc)) % size, 1)
    return jnp.where(masks[TAPS.index((dr, dc))], moved, 0.0)


def sigmoid(v):
    return 1.0 / (1.0 + jnp.exp(-v))


def kernel(
    sizes,
    vol, w1, w2, cot,
    feat, pgrad, g1_out, g2_out,
    h1, x1, tsel, w1big, pool, dsilu_one, w2band, wp, cotf,
    pext, xcol, dext,
    g2f, g2s, g2x, g2yf, g2ys, g2y, g2z, g2r,
    g1s, g1x, g1ys, g1y, g1z, g1r,
    halo_send, halo_recv, xs, xr, ys, yr, zs, zr,
):
    nx, ny, nz, dp_n = sizes
    slabs = nx * ny * nz
    space = lax.axis_index("space")
    dp = lax.axis_index("dp")
    zl = lax.rem(space, nz)
    xy = lax.div(space, nz)
    yi = lax.rem(xy, ny)
    xi = lax.div(xy, ny)
    nxt = lax.rem(space + 1, slabs)
    prv = lax.rem(space + slabs - 1, slabs)
    team = nz * dp_n
    me_z = zl * dp_n + dp

    def x_peer(r):
        other = lax.rem(xi + r, nx)
        return other, ((other * ny + yi) * nz + zl, dp)

    def y_peer(r):
        other = lax.rem(yi + r, ny)
        return other, ((xi * ny + other) * nz + zl, dp)

    def z_peer(r):
        other = lax.rem(me_z + r, team)
        oz = lax.div(other, dp_n)
        return other, oz, (xy * nz + oz, lax.rem(other, dp_n))

    barrier = pltpu.get_barrier_semaphore()
    peers = [(nxt, dp), (prv, dp)]
    peers += [x_peer(r)[1] for r in range(1, nx)]
    peers += [y_peer(r)[1] for r in range(1, ny)]
    peers += [z_peer(r)[2] for r in range(1, team)]
    for peer in peers:
        pl.semaphore_signal(barrier, inc=1, device_id=peer, device_id_type=pl.DeviceIdType.MESH)

    def send(src, dst, ssem, rsem, peer):
        copy = pltpu.make_async_remote_copy(
            src_ref=src, dst_ref=dst, send_sem=ssem, recv_sem=rsem,
            device_id=peer, device_id_type=pl.DeviceIdType.MESH,
        )
        copy.start()
        return copy

    masks_one = tap_masks(32)
    own = jnp.concatenate([vol[p].astype(F32) for p in range(4)], axis=0)
    for v in range(9):
        x1[v * 16:(v + 1) * 16, :] = shifted(own, v, masks_one, 32).astype(BF16)
    x1[224:256, :] = jnp.zeros((32, 1024), BF16)

    pl.semaphore_wait(barrier, len(peers))
    sends = []
    h1_hi = send(vol.at[0], h1.at[0], halo_send.at[0], halo_recv.at[0], (prv, dp))
    h1_lo = send(vol.at[3], h1.at[1], halo_send.at[1], halo_recv.at[1], (nxt, dp))

    k = iota((1, 256), 1)
    is_own = k < 144
    kh = k - 144
    v_k = jnp.where(is_own, k // 16, kh // 8)
    p_k = jnp.where(is_own, (k % 16) // 4 + 1, jnp.where((kh % 8) < 4, 5, 0))
    c_k = k % 4
    row = iota((128, 256), 0)
    for d in range(4):
        kd = p_k - d
        ok = jnp.logical_and(jnp.logical_and(kd >= 0, kd <= 2), k < 216)
        target = jnp.where(ok, c_k * 27 + kd * 9 + v_k, -1)
        tsel[:, d * 256:(d + 1) * 256] = jnp.where(row == target, 1.0, 0.0).astype(BF16)
    for d in range(4):
        w1big[d * 32:(d + 1) * 32, :] = dot(w1[...], tsel[:, d * 256:(d + 1) * 256]).astype(BF16)

    for blk in range(4):
        r = iota((256, 256), 0) + blk * 256
        c = iota((256, 256), 1)
        pool[blk * 256:(blk + 1) * 256, :] = jnp.where(
            c == (r // 64) * 16 + (r % 32) // 2, 1.0, 0.0
        ).astype(BF16)

    zero = jnp.zeros((32, 64), F32)
    for v in range(9):
        w = [w2[kd * 9 + v].astype(F32) for kd in range(3)]
        left = jnp.concatenate([w[0], w[1], w[2], zero], axis=0)
        right = jnp.concatenate([zero, w[0], w[1], w[2]], axis=0)
        both = jnp.concatenate([left, right], axis=1)
        w2band[:, v * 128:(v + 1) * 128] = both.T.astype(BF16)
        top = jnp.concatenate([w[2], w[1], w[0], zero], axis=1)
        bottom = jnp.concatenate([zero, w[2], w[1], w[0]], axis=1)
        wp[v * 64:v * 64 + 32, :] = top.astype(BF16)
        wp[v * 64 + 32:v * 64 + 64, :] = bottom.astype(BF16)
    for d in range(2):
        cotf[d * 64:(d + 1) * 64, :] = cot[d].astype(F32)

    h1_hi.wait()
    h1_lo.wait()
    first = space == 0
    last = space == slabs - 1
    hi = jnp.where(last, 0.0, h1[0].astype(F32))
    lo = jnp.where(first, 0.0, h1[1].astype(F32))
    halo = jnp.concatenate([hi, lo], axis=0)
    parts = [shifted(halo, v, masks_one, 32) for v in range(9)] + [jnp.zeros((8, 1024), F32)]
    for j in range(5):
        x1[144 + 16 * j:160 + 16 * j, :] = jnp.concatenate(
            [parts[2 * j], parts[2 * j + 1]], axis=0
        ).astype(BF16)

    act_hi = []
    act_lo = []
    for dd in range(2):
        total = None
        for d in (2 * dd, 2 * dd + 1):
            pre = dot(w1big[d * 32:(d + 1) * 32, :], x1[...])
            s = sigmoid(pre)
            act = pre * s
            dsilu_one[d * 32:(d + 1) * 32, :] = s * (1.0 + pre * (1.0 - s))
            total = act if total is None else total + act
        high = total.astype(BF16)
        act_hi.append(high)
        act_lo.append((total - high.astype(F32)).astype(BF16))
    sums = dot(jnp.concatenate(act_hi + act_lo, axis=0), pool[...])
    pooled = ((sums[0:64] + sums[64:128]) * 0.125).astype(BF16)
    pext[32:96, :] = pooled
    h2_hi = send(pext.at[32:64], pext.at[96:128], halo_send.at[2], halo_recv.at[2], (prv, dp))
    h2_lo = send(pext.at[64:96], pext.at[0:32], halo_send.at[3], halo_recv.at[3], (nxt, dp))

    masks = tap_masks(16)
    pooled_f = pooled.astype(F32)
    for v in range(9):
        xcol[v * 128 + 32:v * 128 + 96, :] = shifted(pooled_f, v, masks, 16).astype(BF16)
    h2_hi.wait()
    h2_lo.wait()
    hi = jnp.where(last, 0.0, pext[96:128, :].astype(F32))
    lo = jnp.where(first, 0.0, pext[0:32, :].astype(F32))
    for v in range(9):
        xcol[v * 128 + 96:v * 128 + 128, :] = shifted(hi, v, masks, 16).astype(BF16)
        xcol[v * 128:v * 128 + 32, :] = shifted(lo, v, masks, 16).astype(BF16)

    pre = dot(w2band[...], xcol[...])
    s = sigmoid(pre)
    delta = (cotf[...] * (s * (1.0 + pre * (1.0 - s)))).astype(BF16)
    dext[64:192, :] = delta
    h3_hi = send(dext.at[64:128], dext.at[192:256], halo_send.at[4], halo_recv.at[4], (prv, dp))
    h3_lo = send(dext.at[128:192], dext.at[0:64], halo_send.at[5], halo_recv.at[5], (nxt, dp))
    feat[...] = (pre * s).astype(BF16)

    rows_x, rows_y, rows_z = 64 // nx, 64 // (nx * ny), 64 // slabs
    scale_two = 1.0 / 512.0 * math.sqrt(64 * 8 / (slabs * dp_n))
    for v in range(9):
        g = dot_nt(delta, xcol[v * 128:(v + 1) * 128, :])
        g = (g[0:64] + pltpu.roll(g[64:128], 96, 1)) * scale_two
        for i in range(nx):
            piece = g[i * rows_x:(i + 1) * rows_x]
            g2f[i, :, v * 128:(v + 1) * 128] = piece
            g2s[i, :, v * 128:(v + 1) * 128] = piece.astype(BF16)
    g2_x = []
    for r in range(1, nx):
        other, peer = x_peer(r)
        g2_x.append(send(g2s.at[other], g2x.at[r - 1], xs.at[0, r - 1], xr.at[0, r - 1], peer))

    h3_hi.wait()
    h3_lo.wait()
    hi = jnp.where(last, 0.0, dext[192:256, :].astype(F32)).astype(BF16)
    lo = jnp.where(first, 0.0, dext[0:64, :].astype(F32)).astype(BF16)
    z = dot(wp[...], jnp.concatenate([lo, delta, hi], axis=0))
    total = None
    for v in range(9):
        term = shifted(z[v * 64:(v + 1) * 64], v, masks, 16, sign=-1)
        total = term if total is None else total + term
    pg = total.astype(BF16)
    pgrad[...] = pg

    spread = dot_nt(pg, pool[...]) * 0.125
    g1 = None
    for d in range(4):
        dd = d // 2
        one = (spread[dd * 32:(dd + 1) * 32] * dsilu_one[d * 32:(d + 1) * 32, :]).astype(BF16)
        g = dot_nt(one, x1[...])
        hi = g.astype(BF16)
        rest = g - hi.astype(F32)
        mid = rest.astype(BF16)
        low = (rest - mid.astype(F32)).astype(BF16)
        out = dot_nt(jnp.concatenate([hi, mid, low], axis=0), tsel[:, d * 256:(d + 1) * 256])
        out = out[0:32] + (out[32:64] + out[64:96])
        g1 = out if g1 is None else g1 + out
    g1 = g1 * (1.0 / math.sqrt(4096 * slabs * dp_n))
    q_x, q_y = 32 // nx, 32 // (nx * ny)
    for i in range(nx):
        g1s[i] = g1[i * q_x:(i + 1) * q_x]
    g1_x = []
    for r in range(1, nx):
        other, peer = x_peer(r)
        g1_x.append(send(g1s.at[other], g1x.at[r - 1], xs.at[1, r - 1], xr.at[1, r - 1], peer))

    for copy in g2_x:
        copy.wait()
    total = g2f[xi]
    for r in range(nx - 1):
        total = total + g2x[r].astype(F32)
    for i in range(ny):
        piece = total[i * rows_y:(i + 1) * rows_y]
        g2yf[i] = piece
        g2ys[i] = piece.astype(BF16)
    g2_y = []
    for r in range(1, ny):
        other, peer = y_peer(r)
        g2_y.append(send(g2ys.at[other], g2y.at[r - 1], ys.at[0, r - 1], yr.at[0, r - 1], peer))

    for copy in g1_x:
        copy.wait()
    total = g1s[xi]
    for r in range(nx - 1):
        total = total + g1x[r]
    for i in range(ny):
        g1ys[i] = total[i * q_y:(i + 1) * q_y]
    g1_y = []
    for r in range(1, ny):
        other, peer = y_peer(r)
        g1_y.append(send(g1ys.at[other], g1y.at[r - 1], ys.at[1, r - 1], yr.at[1, r - 1], peer))

    for copy in g2_y:
        copy.wait()
    total = g2yf[yi]
    for r in range(ny - 1):
        total = total + g2y[r].astype(F32)
    for i in range(nz):
        g2z[i] = total[i * rows_z:(i + 1) * rows_z]
    g2r[me_z] = g2z[zl]
    g2_z = []
    for r in range(1, team):
        other, oz, peer = z_peer(r)
        g2_z.append(send(g2z.at[oz], g2r.at[me_z], zs.at[0, r - 1], zr.at[0, me_z], peer))

    for copy in g1_y:
        copy.wait()
    total = g1ys[yi]
    for r in range(ny - 1):
        total = total + g1y[r]
    g1z[...] = total
    g1r[me_z] = total
    g1_z = []
    for r in range(1, team):
        other, oz, peer = z_peer(r)
        g1_z.append(send(g1z, g1r.at[me_z], zs.at[1, r - 1], zr.at[1, me_z], peer))

    for r in range(1, team):
        other, oz, peer = z_peer(r)
        g2_z[r - 1].wait_send()
        pltpu.make_async_remote_copy(
            src_ref=g2z.at[zl], dst_ref=g2r.at[other], send_sem=zs.at[0, r - 1],
            recv_sem=zr.at[0, other], device_id=peer, device_id_type=pl.DeviceIdType.MESH,
        ).wait_recv()
    total = g2r[0]
    for r in range(1, team):
        total = total + g2r[r]
    g2_out[...] = total
    for r in range(1, team):
        other, oz, peer = z_peer(r)
        g1_z[r - 1].wait_send()
        pltpu.make_async_remote_copy(
            src_ref=g1z, dst_ref=g1r.at[other], send_sem=zs.at[1, r - 1],
            recv_sem=zr.at[1, other], device_id=peer, device_id_type=pl.DeviceIdType.MESH,
        ).wait_recv()
    total = g1r[0]
    for r in range(1, team):
        total = total + g1r[r]
    g1_out[...] = total


def on_device(sizes, volumes, kernel_one, kernel_two, cotangent):
    nx, ny, nz, dp_n = sizes
    slabs, team = nx * ny * nz, nz * dp_n
    vol = jnp.transpose(volumes[0], (1, 0, 2, 3)).reshape(4, 4, 1024)
    w1 = jnp.pad(kernel_one.reshape(32, 108), ((0, 0), (0, 20)))
    w2 = jnp.transpose(kernel_two, (2, 3, 4, 1, 0)).reshape(27, 32, 64)
    cot = jnp.transpose(cotangent[0], (1, 0, 2))
    rows_x, rows_y, rows_z = 64 // nx, 64 // (nx * ny), 64 // slabs
    q_x, q_y = 32 // nx, 32 // (nx * ny)
    cols = 1152
    vmem = pl.BlockSpec(memory_space=pltpu.VMEM)
    scratch = [
        ((2, 4, 1024), BF16),
        ((256, 1024), BF16),
        ((128, 1024), BF16),
        ((128, 256), BF16),
        ((1024, 256), BF16),
        ((128, 1024), F32),
        ((128, cols), BF16),
        ((576, 256), BF16),
        ((128, 256), F32),
        ((128, 256), BF16),
        ((cols, 256), BF16),
        ((256, 256), BF16),
        ((nx, rows_x, cols), F32),
        ((nx, rows_x, cols), BF16),
        ((nx - 1, rows_x, cols), BF16),
        ((ny, rows_y, cols), F32),
        ((ny, rows_y, cols), BF16),
        ((ny - 1, rows_y, cols), BF16),
        ((nz, rows_z, cols), F32),
        ((team, rows_z, cols), F32),
        ((nx, q_x, 128), F32),
        ((nx - 1, q_x, 128), F32),
        ((ny, q_y, 128), F32),
        ((ny - 1, q_y, 128), F32),
        ((q_y, 128), F32),
        ((team, q_y, 128), F32),
    ]
    dma = pltpu.SemaphoreType.DMA
    feat, pgrad, g1, g2 = pl.pallas_call(
        functools.partial(kernel, sizes),
        out_shape=(
            jax.ShapeDtypeStruct((128, 256), BF16),
            jax.ShapeDtypeStruct((64, 256), BF16),
            jax.ShapeDtypeStruct((q_y, 128), F32),
            jax.ShapeDtypeStruct((rows_z, cols), F32),
        ),
        in_specs=[vmem] * 4,
        out_specs=(vmem,) * 4,
        scratch_shapes=[pltpu.VMEM(shape, dtype) for shape, dtype in scratch] + [
            dma((6,)), dma((6,)),
            dma((2, nx - 1)), dma((2, nx - 1)),
            dma((2, ny - 1)), dma((2, ny - 1)),
            dma((2, team - 1)), dma((2, team)),
        ],
        compiler_params=pltpu.CompilerParams(collective_id=0, has_side_effects=True),
        name="conv_step",
    )(vol, w1, w2, cot)
    features = jnp.transpose(feat.reshape(2, 64, 256), (1, 0, 2))[None]
    pooled_grad = jnp.transpose(pgrad.reshape(2, 32, 256), (1, 0, 2))[None]
    zl = lax.rem(lax.axis_index("space"), nz)
    flat_one = g1[:, :108].reshape(-1)
    half = flat_one.shape[0] // nz
    grad_one = lax.dynamic_slice_in_dim(flat_one, zl * half, half, 0)
    grad_two = jnp.transpose(g2.reshape(rows_z, 9, 4, 32)[:, :, :3], (0, 3, 2, 1)).reshape(-1)
    return features, pooled_grad, grad_one, grad_two


def solution(mesh):
    slabs, dp_n = mesh.shape["space"], mesh.shape["dp"]
    sizes = (4, 8, 2, dp_n) if slabs == 64 else (2, 2, slabs // 4, dp_n)
    in_specs = (P("dp", None, "space", None, None), P(), P(), P("dp", None, "space", None))
    out_specs = (P("dp", None, "space", None), P("dp", None, "space", None), P("space"), P("space"))
    return jax.shard_map(
        functools.partial(on_device, sizes), mesh=mesh, in_specs=in_specs, out_specs=out_specs,
        check_vma=False,
    )
```

time: 372 us -> 53.7 us (0.14)
  waiting for transfers between devices: 130 us -> 0 us
  blocking collectives: 109 us -> 0 us
  local copies, waits for them, and re-layouts: 58.9 us -> 7.73 us
  Pallas kernels: 0 us -> 45 us
  matrix products: 36.6 us -> 0 us
  starting transfers between devices: 16.2 us -> 0 us
  between operations: 14.4 us -> 0.68 us
  other arithmetic: 3.91 us -> 0.02 us
    psum x1 -> x0, waiting for transfers between devices: 125 us -> none  [on_device(): total_one, total_two = lax.psum((flat_one, flat_two), ('space', 'dp'))]
    psum x1 -> x0, blocking collectives: 109 us -> none  [on_device(): total_one, total_two = lax.psum((flat_one, flat_two), ('space', 'dp'))]
    pallas_call x0 -> x1, Pallas kernels: none -> 45 us  [on_device(): pl.pallas_call(functools.partial(kernel, sizes), out_shape=(jax.ShapeDtyp...]
    transpose x3 -> x0, matrix products: 27.8 us -> none  [kernel_term(): return jnp.transpose(result, (1, 0, 2, 3, 4))]
    mul x8 -> x0, local copies, waits for them, and re-layouts: 24.7 us -> none  [the longest x2 23.1 us: on_device(): flat_two = term_two.reshape(-1) * (1.0 / math.sqrt(count // 8))]
    ppermute x6 -> x0, starting transfers between devices: 16.2 us -> none  [the longest x3 12.1 us: extended_2(): lax.ppermute(lax.slice_in_dim(block, block.shape[dim] - width, None, axis...]
    dynamic_slice x14 -> x1, local copies, waits for them, and re-layouts: 10.1 us -> 0.58 us  [on_device(): grad_one = lax.dynamic_slice_in_dim(flat_one, zl * half, half, 0)]
    conv_general_dilated x4 -> x0, matrix products: 8.74 us -> none  [conv_local(): lax.conv_general_dilated(inputs, kernel, (1, 1, 1), [(0, 0), (1, 1), (1,...]
  transfers between devices with their start and end apart: 7 -> 0, of which waited for: 3 -> 0; matrix products, arithmetic and copies ran while one was open for 20% -> 0% of each run, Pallas kernels for 0% -> 0%
where the time goes in v1:
time: 53.7 us; the launch traced here: 53.4 us
  Pallas kernels  45 us (84%)
  local copies, waits for them, and re-layouts  7.73 us (14%)
  between operations  0.68 us (1%)
    pallas_call x1, Pallas kernels, on_device(): pl.pallas_call(functools.partial(kernel, sizes), out_shape=(jax.ShapeDtyp...  45 us
    reshape x2, local copies, waits for them, and re-layouts, on_device(): vol = jnp.transpose(volumes[0], (1, 0, 2, 3)).reshape(4, 4, 1024)  1.71 us
    unnamed x13, local copies, waits for them, and re-layouts  1.66 us
    reshape x1, local copies, waits for them, and re-layouts, on_device(): features = jnp.transpose(feat.reshape(2, 64, 256), (1, 0, 2))[None]  1.54 us

profile of v1, /device:TPU:1, one launch (start us, length us, event | category | flops | bytes accessed | tf_op | source)
XLA Modules:
  0.0 53.4 jit_solution(797026302513665374)
XLA Ops:
  0.6 1.1 %reshape.38 = bf16[4,4,1024]{2,0,1:T(4,128)(2,1)S(1)} reshape(bf16[4,4,32,32]{3,2,0,1:T(8,128)(2,1)} %bitcast.37) | data formatting | bytes 65536 | tf_op jit(solution)/shard_map/reshape | solution.py:335
  1.7 0.0 copy-start.2
  1.7 0.6 %copy.20.vol = bf16[4,4,1024]{2,1,0:T(4,128)(2,1)} copy(bf16[4,4,1024]{2,0,1:T(4,128)(2,1)S(1)} %reshape.38) | data formatting | bytes 65536 | tf_op jit(solution)/shard_map/reshape | solution.py:335
  2.4 0.1 copy-done.2
  2.5 0.0 copy-start
  2.5 0.1 copy.15
  2.6 0.6 %pad.4.w1 = bf16[32,128]{1,0:T(8,128)(2,1)} pad(bf16[32,108]{1,0:T(8,128)(2,1)S(1)} %copy.15, bf16[]{:T(256)} %constant.12.clone.1), padding=0_0x0_20 | pad | bytes 15106 | tf_op jit(solution)/shard_map/jit(_pad)/pad | solution.py:336
  3.2 0.1 copy-done
  3.3 0.6 %copy.26 = bf16[1,64,2,256]{3,1,2,0:T(8,128)(2,1)} copy(bf16[1,64,2,256]{3,2,1,0:T(2,128)(2,1)S(1)} %copy-done) | data formatting | bytes 131072 | tf_op args[3]
  4.0 45.0 %conv_step.1 = (bf16[128,256]{1,0:T(8,128)(2,1)}, bf16[64,256]{1,0:T(8,128)(2,1)}, f32[1,128]{1,0:T(1,128)}, f32[1,1152]{1,0:T(1,128)}) custom-call(bf16[4,4,1024]{2,1,0:T(4,128)(2,1)} %copy.20.vol, bf16[32,128]{1,0:T(8,128)(2,1)} %pad.4.w1, bf16[27,32,64]{2,1,0:T(8,128)(2,1)} %bitcast.36, bf16[2,64,256]{2,1,0:T(8,128)(2,1)} %bitcast.34), custom_call_target="tpu_custom_call" | custom-call | tf_op jit(solution)/shard_map/conv_step/pallas_call | solution.py:372
  48.9 0.0 copy-start.1
  48.9 1.5 %copy.25 = bf16[2,64,256]{2,0,1:T(2,128)(2,1)} copy(bf16[2,64,256]{2,1,0:T(8,128)(2,1)} %bitcast.40) | data formatting | bytes 131072 | tf_op jit(solution)/shard_map/reshape | solution.py:391
  50.5 0.0 copy-done.1
  50.5 0.6 %copy.27 = bf16[2,32,256]{2,0,1:T(2,128)(2,1)} copy(bf16[2,32,256]{2,1,0:T(8,128)(2,1)S(1)} %bitcast.42) | data formatting | bytes 65536 | tf_op jit(solution)/shard_map/reshape | solution.py:392
  51.1 0.0 copy-start.3
  51.1 0.0 copy-start.4
  51.1 0.7 %copy-done.4 = f32[1,128]{1,0:T(1,128)S(1)} copy-done((f32[1,128]{1,0:T(1,128)S(1)}, f32[1,128]{1,0:T(1,128)}, u32[]{:S(2)}) %copy-start.4) | copy-done | bytes 536
  51.8 0.6 %dynamic-slice_bitcast_fusion = f32[54]{0:T(128)} fusion(f32[1,108]{1,0:T(1,128)S(1)} %bitcast.43, s32[]{:T(128)S(6)} %select_n.3), kind=kLoop, calls=%fused_computation.3 | loop fusion | bytes 436 | tf_op jit(solution)/shard_map/dynamic_slice | solution.py:396
  52.4 0.0 copy-done.3
  52.4 0.1 reshape.36
  52.5 0.1 copy.21
  52.6 0.8 %reshape.37 = f32[864]{0:T(1024)} reshape(f32[1,32,3,9]{3,2,1,0:T(4,128)S(1)} %bitcast.35) | data formatting | bytes 6912 | tf_op jit(solution)/shard_map/reshape | solution.py:397
  (3 shorter events, 0.1 us)
Async XLA Ops:
  1.7 0.7 %copy-start.2 = (bf16[32,4,3,3,3]{0,1,4,3,2:T(4,128)(2,1)S(1)}, bf16[32,4,3,3,3]{0,1,4,3,2:T(4,128)(2,1)}, u32[]{:S(2)}) copy-start(bf16[32,4,3,3,3]{0,1,4,3,2:T(4,128)(2,1)} %param.5) | copy-start | bytes 20740
  2.5 0.8 %copy-start = (bf16[1,64,2,256]{3,2,1,0:T(2,128)(2,1)S(1)}, bf16[1,64,2,256]{3,2,1,0:T(2,128)(2,1)}, u32[]{:S(2)}) copy-start(bf16[1,64,2,256]{3,2,1,0:T(2,128)(2,1)} %param.7) | copy-start | bytes 196612
  48.9 1.6 %copy-start.1 = (bf16[64,256]{1,0:T(8,128)(2,1)S(1)}, bf16[64,256]{1,0:T(8,128)(2,1)}, u32[]{:S(2)}) copy-start(bf16[64,256]{1,0:T(8,128)(2,1)} %get-tuple-element.9) | copy-start | bytes 98308
  51.1 1.3 %copy-start.3 = (f32[1,1152]{1,0:T(1,128)S(1)}, f32[1,1152]{1,0:T(1,128)}, u32[]{:S(2)}) copy-start(f32[1,1152]{1,0:T(1,128)} %get-tuple-element.11) | copy-start | bytes 13828
  51.1 0.7 %copy-start.4 = (f32[1,128]{1,0:T(1,128)S(1)}, f32[1,128]{1,0:T(1,128)}, u32[]{:S(2)}) copy-start(f32[1,128]{1,0:T(1,128)} %get-tuple-element.10) | copy-start | bytes 1540

commit v2 on v1

--- a/solution.py
+++ b/solution.py
@@ -51,19 +51,25 @@
     return jnp.where(masks[TAPS.index((dr, dc))], moved, 0.0)
 
 
+def one_hot(shape, column_of_row):
+    return jnp.where(iota(shape, 1) == column_of_row(iota(shape, 0)), 1.0, 0.0).astype(BF16)
+
+
 def sigmoid(v):
     return 1.0 / (1.0 + jnp.exp(-v))
 
 
 def kernel(
     sizes,
-    vol, w1, w2, cot,
-    feat, pgrad, g1_out, g2_out,
-    h1, x1, tsel, w1big, pool, dsilu_one, w2band, wp, cotf,
-    pext, xcol, dext,
+    vol_in, w1_in, w2_in, cot_in,
+    feat_out, pgrad_out, g1_out, g2_out,
+    vol, w1, w2, cot, feat, pgrad,
+    vrows, vgrp, vnear, vedge, vfar, cots, cotr, w1rows,
+    x1, tsel, w1big, pool, dsilu_one, w2band, wp,
+    xcol_a, xcol_b,
     g2f, g2s, g2x, g2yf, g2ys, g2y, g2z, g2r,
     g1s, g1x, g1ys, g1y, g1z, g1r,
-    halo_send, halo_recv, xs, xr, ys, yr, zs, zr,
+    local, halo_send, halo_recv, xs, xr, ys, yr, zs, zr,
 ):
     nx, ny, nz, dp_n = sizes
     slabs = nx * ny * nz
@@ -75,6 +81,8 @@
     xi = lax.div(xy, ny)
     nxt = lax.rem(space + 1, slabs)
     prv = lax.rem(space + slabs - 1, slabs)
+    nxt2 = lax.rem(space + 2, slabs)
+    prv2 = lax.rem(space + slabs - 2, slabs)
     team = nz * dp_n
     me_z = zl * dp_n + dp
 
@@ -92,12 +100,19 @@
         return other, oz, (xy * nz + oz, lax.rem(other, dp_n))
 
     barrier = pltpu.get_barrier_semaphore()
-    peers = [(nxt, dp), (prv, dp)]
+    peers = [(nxt, dp), (prv, dp), (nxt2, dp), (prv2, dp)]
     peers += [x_peer(r)[1] for r in range(1, nx)]
     peers += [y_peer(r)[1] for r in range(1, ny)]
     peers += [z_peer(r)[2] for r in range(1, team)]
     for peer in peers:
         pl.semaphore_signal(barrier, inc=1, device_id=peer, device_id_type=pl.DeviceIdType.MESH)
+
+    loads = [
+        pltpu.make_async_copy(src, dst, local.at[i])
+        for i, (src, dst) in enumerate([(vol_in, vol), (cot_in, cot), (w1_in, w1), (w2_in, w2)])
+    ]
+    for copy in loads:
+        copy.start()
 
     def send(src, dst, ssem, rsem, peer):
         copy = pltpu.make_async_remote_copy(
@@ -107,16 +122,43 @@
         copy.start()
         return copy
 
+    loads[0].wait()
+    for p in range(4):
+        for c in range(4):
+            vrows[(p * 4 + c) * 32:(p * 4 + c) * 32 + 32, :] = vol[c, p].astype(F32)
+    own = jnp.concatenate(
+        [
+            jnp.concatenate([vrows[pl.ds(4 * j + k, 16, stride=32), :] for k in range(4)], axis=1)
+            for j in range(8)
+        ],
+        axis=1,
+    )
+    vgrp[...] = own.astype(BF16)
+    vedge[0] = own[0:4].astype(BF16)
+    vedge[1] = own[12:16].astype(BF16)
+    loads[1].wait()
+    split = one_hot((128, 128), lambda r: (r % 64) * 2 + r // 64)
+    merge = one_hot((128, 128), lambda r: (r % 2) * 64 + r // 2)
+    merge_half = one_hot((64, 64), lambda r: (r % 2) * 32 + r // 2)
+    own_cot = dot(split, cot[...].reshape(128, 256))
+    cots[0] = own_cot[0:64].astype(BF16)
+    cots[1] = own_cot[64:128].astype(BF16)
+
+    pl.semaphore_wait(barrier, len(peers))
+    halos = [
+        send(vgrp, vnear.at[0], halo_send.at[0], halo_recv.at[0], (nxt, dp)),
+        send(vgrp, vnear.at[1], halo_send.at[1], halo_recv.at[1], (prv, dp)),
+        send(vedge.at[1], vfar.at[0], halo_send.at[2], halo_recv.at[2], (nxt2, dp)),
+        send(vedge.at[0], vfar.at[1], halo_send.at[3], halo_recv.at[3], (prv2, dp)),
+        send(cots.at[1], cotr.at[0], halo_send.at[4], halo_recv.at[4], (nxt, dp)),
+        send(cots.at[0], cotr.at[1], halo_send.at[5], halo_recv.at[5], (prv, dp)),
+    ]
+
     masks_one = tap_masks(32)
-    own = jnp.concatenate([vol[p].astype(F32) for p in range(4)], axis=0)
     for v in range(9):
-        x1[v * 16:(v + 1) * 16, :] = shifted(own, v, masks_one, 32).astype(BF16)
-    x1[224:256, :] = jnp.zeros((32, 1024), BF16)
-
-    pl.semaphore_wait(barrier, len(peers))
-    sends = []
-    h1_hi = send(vol.at[0], h1.at[0], halo_send.at[0], halo_recv.at[0], (prv, dp))
-    h1_lo = send(vol.at[3], h1.at[1], halo_send.at[1], halo_recv.at[1], (nxt, dp))
+        x1[1, v * 16:(v + 1) * 16, :] = shifted(own, v, masks_one, 32).astype(BF16)
+    for g in range(3):
+        x1[g, 224:256, :] = jnp.zeros((32, 1024), BF16)
 
     k = iota((1, 256), 1)
     is_own = k < 144
@@ -130,16 +172,22 @@
         ok = jnp.logical_and(jnp.logical_and(kd >= 0, kd <= 2), k < 216)
         target = jnp.where(ok, c_k * 27 + kd * 9 + v_k, -1)
         tsel[:, d * 256:(d + 1) * 256] = jnp.where(row == target, 1.0, 0.0).astype(BF16)
+    w1rows[...] = jnp.zeros((128, 128), F32)
+    loads[2].wait()
+    for t in range(27):
+        w1rows[pl.ds(t, 4, stride=27), 0:32] = w1[t].astype(F32)
+    w1t = w1rows[...].T[0:32].astype(BF16)
+    bands = dot(w1t, tsel[...]).astype(BF16)
     for d in range(4):
-        w1big[d * 32:(d + 1) * 32, :] = dot(w1[...], tsel[:, d * 256:(d + 1) * 256]).astype(BF16)
+        w1big[d * 32:(d + 1) * 32, :] = bands[:, d * 256:(d + 1) * 256]
 
     for blk in range(4):
         r = iota((256, 256), 0) + blk * 256
-        c = iota((256, 256), 1)
         pool[blk * 256:(blk + 1) * 256, :] = jnp.where(
-            c == (r // 64) * 16 + (r % 32) // 2, 1.0, 0.0
+            iota((256, 256), 1) == (r // 64) * 16 + (r % 32) // 2, 1.0, 0.0
         ).astype(BF16)
 
+    loads[3].wait()
     zero = jnp.zeros((32, 64), F32)
     for v in range(9):
         w = [w2[kd * 9 + v].astype(F32) for kd in range(3)]
@@ -151,66 +199,81 @@
         bottom = jnp.concatenate([zero, w[2], w[1], w[0]], axis=1)
         wp[v * 64:v * 64 + 32, :] = top.astype(BF16)
         wp[v * 64 + 32:v * 64 + 64, :] = bottom.astype(BF16)
-    for d in range(2):
-        cotf[d * 64:(d + 1) * 64, :] = cot[d].astype(F32)
-
-    h1_hi.wait()
-    h1_lo.wait()
-    first = space == 0
-    last = space == slabs - 1
-    hi = jnp.where(last, 0.0, h1[0].astype(F32))
-    lo = jnp.where(first, 0.0, h1[1].astype(F32))
-    halo = jnp.concatenate([hi, lo], axis=0)
-    parts = [shifted(halo, v, masks_one, 32) for v in range(9)] + [jnp.zeros((8, 1024), F32)]
-    for j in range(5):
-        x1[144 + 16 * j:160 + 16 * j, :] = jnp.concatenate(
-            [parts[2 * j], parts[2 * j + 1]], axis=0
-        ).astype(BF16)
-
-    act_hi = []
-    act_lo = []
-    for dd in range(2):
-        total = None
-        for d in (2 * dd, 2 * dd + 1):
-            pre = dot(w1big[d * 32:(d + 1) * 32, :], x1[...])
+
+    for copy in halos[0:4]:
+        copy.wait()
+    first, last = space == 0, space == slabs - 1
+    groups = [
+        jnp.where(first, 0.0, vnear[0].astype(F32)),
+        own,
+        jnp.where(last, 0.0, vnear[1].astype(F32)),
+    ]
+    far_lo = jnp.where(space <= 1, 0.0, vfar[0].astype(F32))
+    far_hi = jnp.where(space >= slabs - 2, 0.0, vfar[1].astype(F32))
+    below = [far_lo, groups[0][12:16], own[12:16]]
+    above = [own[0:4], groups[2][0:4], far_hi]
+    masks = tap_masks(16)
+    for g in (0, 2, 1):
+        if g != 1:
+            for v in range(9):
+                x1[g, v * 16:(v + 1) * 16, :] = shifted(groups[g], v, masks_one, 32).astype(BF16)
+        halo = jnp.concatenate([above[g], below[g]], axis=0)
+        parts = [shifted(halo, v, masks_one, 32) for v in range(9)] + [jnp.zeros((8, 1024), F32)]
+        for j in range(5):
+            x1[g, 144 + 16 * j:160 + 16 * j, :] = jnp.concatenate(
+                [parts[2 * j], parts[2 * j + 1]], axis=0
+            ).astype(BF16)
+        sums = None
+        for n in range(4):
+            lanes = slice(n * 256, (n + 1) * 256)
+            pre = dot(w1big[...], x1[g, :, lanes])
             s = sigmoid(pre)
             act = pre * s
-            dsilu_one[d * 32:(d + 1) * 32, :] = s * (1.0 + pre * (1.0 - s))
-            total = act if total is None else total + act
-        high = total.astype(BF16)
-        act_hi.append(high)
-        act_lo.append((total - high.astype(F32)).astype(BF16))
-    sums = dot(jnp.concatenate(act_hi + act_lo, axis=0), pool[...])
-    pooled = ((sums[0:64] + sums[64:128]) * 0.125).astype(BF16)
-    pext[32:96, :] = pooled
-    h2_hi = send(pext.at[32:64], pext.at[96:128], halo_send.at[2], halo_recv.at[2], (prv, dp))
-    h2_lo = send(pext.at[64:96], pext.at[0:32], halo_send.at[3], halo_recv.at[3], (nxt, dp))
-
-    masks = tap_masks(16)
-    pooled_f = pooled.astype(F32)
-    for v in range(9):
-        xcol[v * 128 + 32:v * 128 + 96, :] = shifted(pooled_f, v, masks, 16).astype(BF16)
-    h2_hi.wait()
-    h2_lo.wait()
-    hi = jnp.where(last, 0.0, pext[96:128, :].astype(F32))
-    lo = jnp.where(first, 0.0, pext[0:32, :].astype(F32))
-    for v in range(9):
-        xcol[v * 128 + 96:v * 128 + 128, :] = shifted(hi, v, masks, 16).astype(BF16)
-        xcol[v * 128:v * 128 + 32, :] = shifted(lo, v, masks, 16).astype(BF16)
-
-    pre = dot(w2band[...], xcol[...])
-    s = sigmoid(pre)
-    delta = (cotf[...] * (s * (1.0 + pre * (1.0 - s)))).astype(BF16)
-    dext[64:192, :] = delta
-    h3_hi = send(dext.at[64:128], dext.at[192:256], halo_send.at[4], halo_recv.at[4], (prv, dp))
-    h3_lo = send(dext.at[128:192], dext.at[0:64], halo_send.at[5], halo_recv.at[5], (nxt, dp))
-    feat[...] = (pre * s).astype(BF16)
+            if g == 1:
+                dsilu_one[:, lanes] = s * (1.0 + pre * (1.0 - s))
+            total = jnp.concatenate([act[0:32] + act[32:64], act[64:96] + act[96:128]], axis=0)
+            high = total.astype(BF16)
+            low = (total - high.astype(F32)).astype(BF16)
+            part = dot(jnp.concatenate([high, low], axis=0), pool[lanes, :])
+            sums = part if sums is None else sums + part
+        pooled = ((sums[0:64] + sums[64:128]) * 0.125).astype(BF16).astype(F32)
+        if g == 0:
+            pooled = jnp.where(first, 0.0, pooled)
+        if g == 2:
+            pooled = jnp.where(last, 0.0, pooled)
+        for v in range(9):
+            block = shifted(pooled, v, masks, 16).astype(BF16)
+            if g < 2:
+                xcol_a[v * 128 + g * 64:v * 128 + g * 64 + 64, :] = block
+            if g > 0:
+                xcol_b[v * 128 + g * 64 - 64:v * 128 + g * 64, :] = block
+
+    halos[4].wait()
+    halos[5].wait()
+    cot_a = jnp.concatenate([cotr[0].astype(F32), cots[0].astype(F32)], axis=0)
+    cot_b = jnp.concatenate([cots[1].astype(F32), cotr[1].astype(F32)], axis=0)
+    pre_a = dot(w2band[...], xcol_a[...])
+    s_a = sigmoid(pre_a)
+    delta_a = cot_a * (s_a * (1.0 + pre_a * (1.0 - s_a)))
+    pre_b = dot(w2band[...], xcol_b[...])
+    s_b = sigmoid(pre_b)
+    delta_b = cot_b * (s_b * (1.0 + pre_b * (1.0 - s_b)))
+    delta = jnp.concatenate(
+        [
+            jnp.where(first, 0.0, delta_a[0:64]),
+            delta_a[64:128],
+            delta_b[0:64],
+            jnp.where(last, 0.0, delta_b[64:128]),
+        ],
+        axis=0,
+    ).astype(BF16)
 
     rows_x, rows_y, rows_z = 64 // nx, 64 // (nx * ny), 64 // slabs
     scale_two = 1.0 / 512.0 * math.sqrt(64 * 8 / (slabs * dp_n))
     for v in range(9):
-        g = dot_nt(delta, xcol[v * 128:(v + 1) * 128, :])
-        g = (g[0:64] + pltpu.roll(g[64:128], 96, 1)) * scale_two
+        lower = dot_nt(delta[64:128], xcol_a[v * 128:(v + 1) * 128, :])
+        upper = dot_nt(delta[128:192], xcol_b[v * 128:(v + 1) * 128, :])
+        g = (pltpu.roll(lower, 96, 1) + upper) * scale_two
         for i in range(nx):
             piece = g[i * rows_x:(i + 1) * rows_x]
             g2f[i, :, v * 128:(v + 1) * 128] = piece
@@ -220,32 +283,29 @@
         other, peer = x_peer(r)
         g2_x.append(send(g2s.at[other], g2x.at[r - 1], xs.at[0, r - 1], xr.at[0, r - 1], peer))
 
-    h3_hi.wait()
-    h3_lo.wait()
-    hi = jnp.where(last, 0.0, dext[192:256, :].astype(F32)).astype(BF16)
-    lo = jnp.where(first, 0.0, dext[0:64, :].astype(F32)).astype(BF16)
-    z = dot(wp[...], jnp.concatenate([lo, delta, hi], axis=0))
+    z = dot(wp[...], delta)
     total = None
     for v in range(9):
         term = shifted(z[v * 64:(v + 1) * 64], v, masks, 16, sign=-1)
         total = term if total is None else total + term
     pg = total.astype(BF16)
-    pgrad[...] = pg
-
-    spread = dot_nt(pg, pool[...]) * 0.125
+
+    g1k = None
+    for n in range(4):
+        lanes = slice(n * 256, (n + 1) * 256)
+        spread = dot_nt(pg, pool[lanes, :]) * 0.125
+        twice = jnp.concatenate([spread[0:32], spread[0:32], spread[32:64], spread[32:64]], axis=0)
+        one = (twice * dsilu_one[:, lanes]).astype(BF16)
+        part = dot_nt(one, x1[1, :, lanes])
+        g1k = part if g1k is None else g1k + part
+    hi = g1k.astype(BF16)
+    mid = (g1k - hi.astype(F32)).astype(BF16)
     g1 = None
     for d in range(4):
-        dd = d // 2
-        one = (spread[dd * 32:(dd + 1) * 32] * dsilu_one[d * 32:(d + 1) * 32, :]).astype(BF16)
-        g = dot_nt(one, x1[...])
-        hi = g.astype(BF16)
-        rest = g - hi.astype(F32)
-        mid = rest.astype(BF16)
-        low = (rest - mid.astype(F32)).astype(BF16)
-        out = dot_nt(jnp.concatenate([hi, mid, low], axis=0), tsel[:, d * 256:(d + 1) * 256])
-        out = out[0:32] + (out[32:64] + out[64:96])
+        rows = slice(d * 32, (d + 1) * 32)
+        out = dot_nt(jnp.concatenate([hi[rows], mid[rows]], axis=0), tsel[:, d * 256:(d + 1) * 256])
         g1 = out if g1 is None else g1 + out
-    g1 = g1 * (1.0 / math.sqrt(4096 * slabs * dp_n))
+    g1 = (g1[0:32] + g1[32:64]) * (1.0 / math.sqrt(4096 * slabs * dp_n))
     q_x, q_y = 32 // nx, 32 // (nx * ny)
     for i in range(nx):
         g1s[i] = g1[i * q_x:(i + 1) * q_x]
@@ -253,6 +313,16 @@
     for r in range(1, nx):
         other, peer = x_peer(r)
         g1_x.append(send(g1s.at[other], g1x.at[r - 1], xs.at[1, r - 1], xr.at[1, r - 1], peer))
+
+    own_feat = jnp.concatenate([(pre_a * s_a)[64:128], (pre_b * s_b)[0:64]], axis=0).astype(BF16)
+    feat[...] = dot(merge, own_feat).astype(BF16).reshape(64, 2, 256)
+    pgrad[...] = dot(merge_half, pg).astype(BF16).reshape(32, 2, 256)
+    stores = [
+        pltpu.make_async_copy(feat, feat_out, local.at[4]),
+        pltpu.make_async_copy(pgrad, pgrad_out, local.at[5]),
+    ]
+    for copy in stores:
+        copy.start()
 
     for copy in g2_x:
         copy.wait()
@@ -327,32 +397,44 @@
     for r in range(1, team):
         total = total + g1r[r]
     g1_out[...] = total
+    for copy in stores:
+        copy.wait()
 
 
 def on_device(sizes, volumes, kernel_one, kernel_two, cotangent):
     nx, ny, nz, dp_n = sizes
     slabs, team = nx * ny * nz, nz * dp_n
-    vol = jnp.transpose(volumes[0], (1, 0, 2, 3)).reshape(4, 4, 1024)
-    w1 = jnp.pad(kernel_one.reshape(32, 108), ((0, 0), (0, 20)))
+    w1 = jnp.transpose(kernel_one, (2, 3, 4, 1, 0)).reshape(27, 4, 32)
     w2 = jnp.transpose(kernel_two, (2, 3, 4, 1, 0)).reshape(27, 32, 64)
-    cot = jnp.transpose(cotangent[0], (1, 0, 2))
     rows_x, rows_y, rows_z = 64 // nx, 64 // (nx * ny), 64 // slabs
     q_x, q_y = 32 // nx, 32 // (nx * ny)
     cols = 1152
     vmem = pl.BlockSpec(memory_space=pltpu.VMEM)
+    hbm = pl.BlockSpec(memory_space=pl.ANY)
     scratch = [
+        ((4, 4, 32, 32), BF16),
+        ((27, 4, 32), BF16),
+        ((27, 32, 64), BF16),
+        ((64, 2, 256), BF16),
+        ((64, 2, 256), BF16),
+        ((32, 2, 256), BF16),
+        ((512, 32), F32),
+        ((16, 1024), BF16),
+        ((2, 16, 1024), BF16),
         ((2, 4, 1024), BF16),
-        ((256, 1024), BF16),
+        ((2, 4, 1024), BF16),
+        ((2, 64, 256), BF16),
+        ((2, 64, 256), BF16),
+        ((128, 128), F32),
+        ((3, 256, 1024), BF16),
         ((128, 1024), BF16),
         ((128, 256), BF16),
         ((1024, 256), BF16),
         ((128, 1024), F32),
         ((128, cols), BF16),
         ((576, 256), BF16),
-        ((128, 256), F32),
-        ((128, 256), BF16),
         ((cols, 256), BF16),
-        ((256, 256), BF16),
+        ((cols, 256), BF16),
         ((nx, rows_x, cols), F32),
         ((nx, rows_x, cols), BF16),
         ((nx - 1, rows_x, cols), BF16),
@@ -369,33 +451,31 @@
         ((team, q_y, 128), F32),
     ]
     dma = pltpu.SemaphoreType.DMA
-    feat, pgrad, g1, g2 = pl.pallas_call(
+    features, pooled_grad, g1, g2 = pl.pallas_call(
         functools.partial(kernel, sizes),
         out_shape=(
-            jax.ShapeDtypeStruct((128, 256), BF16),
-            jax.ShapeDtypeStruct((64, 256), BF16),
+            jax.ShapeDtypeStruct((64, 2, 256), BF16),
+            jax.ShapeDtypeStruct((32, 2, 256), BF16),
             jax.ShapeDtypeStruct((q_y, 128), F32),
             jax.ShapeDtypeStruct((rows_z, cols), F32),
         ),
-        in_specs=[vmem] * 4,
-        out_specs=(vmem,) * 4,
+        in_specs=[hbm] * 4,
+        out_specs=(hbm, hbm, vmem, vmem),
         scratch_shapes=[pltpu.VMEM(shape, dtype) for shape, dtype in scratch] + [
-            dma((6,)), dma((6,)),
+            dma((6,)), dma((6,)), dma((6,)),
             dma((2, nx - 1)), dma((2, nx - 1)),
             dma((2, ny - 1)), dma((2, ny - 1)),
             dma((2, team - 1)), dma((2, team)),
         ],
         compiler_params=pltpu.CompilerParams(collective_id=0, has_side_effects=True),
         name="conv_step",
-    )(vol, w1, w2, cot)
-    features = jnp.transpose(feat.reshape(2, 64, 256), (1, 0, 2))[None]
-    pooled_grad = jnp.transpose(pgrad.reshape(2, 32, 256), (1, 0, 2))[None]
+    )(volumes[0], w1, w2, cotangent[0])
     zl = lax.rem(lax.axis_index("space"), nz)
     flat_one = g1[:, :108].reshape(-1)
     half = flat_one.shape[0] // nz
     grad_one = lax.dynamic_slice_in_dim(flat_one, zl * half, half, 0)
     grad_two = jnp.transpose(g2.reshape(rows_z, 9, 4, 32)[:, :, :3], (0, 3, 2, 1)).reshape(-1)
-    return features, pooled_grad, grad_one, grad_two
+    return features[None], pooled_grad[None], grad_one, grad_two
 
 
 def solution(mesh):

time: 53.7 us -> 43 us (0.80)
  Pallas kernels: 45 us -> 38.4 us
  local copies, waits for them, and re-layouts: 7.73 us -> 3.68 us
    pallas_call x1, Pallas kernels: 45 us -> 38.4 us  [on_device(): pl.pallas_call(functools.partial(kernel, sizes), out_shape=(jax.ShapeDtyp...]
    reshape x6 -> x0, local copies, waits for them, and re-layouts: 4.01 us -> none  [the longest x2 1.71 us: on_device(): vol = jnp.transpose(volumes[0], (1, 0, 2, 3)).reshape(4, 4, 1024)]
    pad x1 -> x0, local copies, waits for them, and re-layouts: 0.62 us -> none  [on_device(): w1 = jnp.pad(kernel_one.reshape(32, 108), ((0, 0), (0, 20)))]
    unnamed x13 -> x11, local copies, waits for them, and re-layouts: 1.66 us -> 2.24 us
where the time goes in v2:
time: 43 us; the launch traced here: 42.7 us
  Pallas kernels  38.4 us (89%)
  local copies, waits for them, and re-layouts  3.68 us (9%)
  between operations  0.66 us (2%)
    pallas_call x1, Pallas kernels, on_device(): pl.pallas_call(functools.partial(kernel, sizes), out_shape=(jax.ShapeDtyp...  38.4 us
    unnamed x11, local copies, waits for them, and re-layouts  2.24 us

profile of v2, /device:TPU:1, one launch (start us, length us, event | category | flops | bytes accessed | tf_op | source)
XLA Modules:
  0.0 42.7 jit_solution(15069835164102250925)
XLA Ops:
  0.6 38.4 %conv_step.1 = (bf16[64,2,256]{2,1,0:T(2,128)(2,1)}, bf16[32,2,256]{2,1,0:T(2,128)(2,1)}, f32[1,128]{1,0:T(1,128)}, f32[1,1152]{1,0:T(1,128)}) custom-call(bf16[4,4,32,32]{3,2,1,0:T(8,128)(2,1)} %bitcast.17, bf16[27,4,32]{2,1,0:T(4,128)(2,1)} %bitcast.22, bf16[27,32,64]{2,1,0:T(8,128)(2,1)} %bitcast.16, bf16[64,2,256]{2,1,0:T(2,128)(2,1)} %bitcast.19), custom_call_target="tpu_custom_call" | custom-call | tf_op jit(solution)/shard_map/conv_step/pallas_call | solution.py:454
  39.0 0.0 copy-start.3
  39.0 0.6 %copy-done.3 = f32[1,128]{1,0:T(1,128)S(1)} copy-done((f32[1,128]{1,0:T(1,128)S(1)}, f32[1,128]{1,0:T(1,128)}, u32[]{:S(2)}) %copy-start.3) | copy-done | bytes 536
  39.7 0.0 copy-start.2
  39.7 0.6 %dynamic-slice_bitcast_fusion = f32[54]{0:T(128)} fusion(f32[1,108]{1,0:T(1,128)S(1)} %bitcast.23, s32[]{:T(128)S(6)} %select_n.3), kind=kLoop, calls=%fused_computation | loop fusion | bytes 436 | tf_op jit(solution)/shard_map/dynamic_slice | solution.py:476
  40.3 0.1 copy-done.2
  40.4 0.1 reshape.24
  40.5 0.0 copy-start
  40.5 0.1 copy.9
  40.6 0.8 %reshape.25 = f32[864]{0:T(1024)} reshape(f32[1,32,3,9]{3,2,1,0:T(4,128)S(1)} %bitcast.15) | data formatting | bytes 6912 | tf_op jit(solution)/shard_map/reshape | solution.py:477
  41.4 0.0 copy-done
  41.4 0.0 copy-start.1
  41.4 0.6 %copy.12 = bf16[1,64,2,256]{3,2,1,0:T(2,128)(2,1)} copy(bf16[1,64,2,256]{3,2,1,0:T(2,128)(2,1)S(1)} %bitcast.20) | data formatting | bytes 131072
  42.0 0.1 copy-done.1
  42.1 0.6 %copy.13 = bf16[1,32,2,256]{3,2,1,0:T(2,128)(2,1)} copy(bf16[1,32,2,256]{3,2,1,0:T(2,128)(2,1)S(1)} %bitcast.21) | data formatting | bytes 65536
  (1 shorter events, 0.0 us)
Async XLA Ops:
  39.0 0.7 %copy-start.3 = (f32[1,128]{1,0:T(1,128)S(1)}, f32[1,128]{1,0:T(1,128)}, u32[]{:S(2)}) copy-start(f32[1,128]{1,0:T(1,128)} %get-tuple-element.10) | copy-start | bytes 1540
  39.7 0.7 %copy-start.2 = (f32[1,1152]{1,0:T(1,128)S(1)}, f32[1,1152]{1,0:T(1,128)}, u32[]{:S(2)}) copy-start(f32[1,1152]{1,0:T(1,128)} %get-tuple-element.11) | copy-start | bytes 13828
  40.5 0.9 %copy-start = (bf16[64,2,256]{2,1,0:T(2,128)(2,1)S(1)}, bf16[64,2,256]{2,1,0:T(2,128)(2,1)}, u32[]{:S(2)}) copy-start(bf16[64,2,256]{2,1,0:T(2,128)(2,1)} %get-tuple-element.8) | copy-start | bytes 196612
  41.4 0.8 %copy-start.1 = (bf16[32,2,256]{2,1,0:T(2,128)(2,1)S(1)}, bf16[32,2,256]{2,1,0:T(2,128)(2,1)}, u32[]{:S(2)}) copy-start(bf16[32,2,256]{2,1,0:T(2,128)(2,1)} %get-tuple-element.9) | copy-start | bytes 98308

commit v3 on v2

v3 whole, which is shorter than its diff:
```python
import functools
import math

import jax
import jax.numpy as jnp
from jax import lax
from jax.experimental import pallas as pl
from jax.experimental.pallas import tpu as pltpu
from jax.sharding import PartitionSpec as P

F32 = jnp.float32
BF16 = jnp.bfloat16
TAPS = [(a, b) for a in (-1, 0, 1) for b in (-1, 0, 1)]
NT = (((1,), (1,)), ((), ()))


def dot(a, b):
    return jnp.dot(a, b, preferred_element_type=F32)


def dot_nt(a, b):
    return lax.dot_general(a, b, NT, preferred_element_type=F32)


def iota(shape, dim):
    return lax.broadcasted_iota(jnp.int32, shape, dim)


def tap_masks(width):
    lane = iota((1, width * width), 1)
    row, col = lane // width, lane % width
    rows = {-1: row >= 1, 0: None, 1: row < width - 1}
    cols = {-1: col >= 1, 0: None, 1: col < width - 1}
    masks = []
    for dr, dc in TAPS:
        parts = [m for m in (rows[dr], cols[dc]) if m is not None]
        mask = None
        for part in parts:
            mask = part if mask is None else jnp.logical_and(mask, part)
        masks.append(mask)
    return masks


def shifted(block, tap, masks, width, sign=1):
    dr, dc = TAPS[tap]
    dr, dc = sign * dr, sign * dc
    if dr == 0 and dc == 0:
        return block
    size = width * width
    moved = pltpu.roll(block, (-(dr * width + dc)) % size, 1)
    return jnp.where(masks[TAPS.index((dr, dc))], moved, jnp.zeros_like(moved))


def one_hot(shape, column_of_row):
    return jnp.where(iota(shape, 1) == column_of_row(iota(shape, 0)), 1.0, 0.0).astype(BF16)


def silu_parts(half):
    t = jnp.tanh(half)
    return half + half * t, 0.5 + 0.5 * t


def kernel(
    sizes, cols,
    vol_in, w1_in, w2_in, cot_in,
    feat, pgrad, g1_out, g2_out,
    vol, w1, w2, cot,
    vrows, planes, cots, cotr, w1rows,
    x1, tsel, w1big, pool, dsilu_one, w2band, wp, place,
    xcol_a, xcol_b,
    g2s, g2x, g2z, g2r,
    g1s, g1x, g1z, g1r,
    local, halo_send, halo_recv, xs, xr, zs, zr,
):
    nx, ny, nz, dp_n = sizes
    slabs = nx * ny * nz
    space = lax.axis_index("space")
    dp = lax.axis_index("dp")
    zl = lax.rem(space, nz)
    xy = lax.div(space, nz)
    tiles_n = nx * ny
    nxt = lax.rem(space + 1, slabs)
    prv = lax.rem(space + slabs - 1, slabs)
    nxt2 = lax.rem(space + 2, slabs)
    prv2 = lax.rem(space + slabs - 2, slabs)
    team = nz * dp_n
    me_z = zl * dp_n + dp

    def xy_peer(r):
        other = lax.rem(xy + r, tiles_n)
        return other, (other * nz + zl, dp)

    def z_peer(r):
        other = lax.rem(me_z + r, team)
        oz = lax.div(other, dp_n)
        return other, oz, (xy * nz + oz, lax.rem(other, dp_n))

    loads = [
        pltpu.make_async_copy(src, dst, local.at[i])
        for i, (src, dst) in enumerate([(vol_in, vol), (cot_in, cot), (w1_in, w1), (w2_in, w2)])
    ]
    for copy in loads:
        copy.start()
    barrier = pltpu.get_barrier_semaphore()
    peers = [(nxt, dp), (prv, dp), (nxt2, dp), (prv2, dp)]
    peers += [xy_peer(r)[1] for r in range(1, tiles_n)]
    peers += [z_peer(r)[2] for r in range(1, team)]
    for peer in peers:
        pl.semaphore_signal(barrier, inc=1, device_id=peer, device_id_type=pl.DeviceIdType.MESH)

    def send(src, dst, ssem, rsem, peer):
        copy = pltpu.make_async_remote_copy(
            src_ref=src, dst_ref=dst, send_sem=ssem, recv_sem=rsem,
            device_id=peer, device_id_type=pl.DeviceIdType.MESH,
        )
        copy.start()
        return copy

    loads[0].wait()
    for p in range(4):
        for c in range(4):
            vrows[(p * 4 + c) * 32:(p * 4 + c) * 32 + 32, :] = vol[c, p].astype(F32)
    own = jnp.concatenate(
        [
            jnp.concatenate([vrows[pl.ds(4 * j + k, 16, stride=32), :] for k in range(4)], axis=1)
            for j in range(8)
        ],
        axis=1,
    )
    planes[5:9] = own.astype(BF16).reshape(4, 4, 1024)
    planes[14:16] = jnp.zeros((2, 4, 1024), BF16)
    loads[1].wait()
    split = one_hot((128, 128), lambda r: (r % 64) * 2 + r // 64)
    merge = one_hot((128, 128), lambda r: (r % 2) * 64 + r // 2)
    merge_half = one_hot((64, 64), lambda r: (r % 2) * 32 + r // 2)
    own_cot = dot(split, cot[...].reshape(128, 256))
    cots[0] = own_cot[0:64].astype(BF16)
    cots[1] = own_cot[64:128].astype(BF16)

    pl.semaphore_wait(barrier, len(peers))
    halos = [
        send(planes.at[5:9], planes.at[1:5], halo_send.at[0], halo_recv.at[0], (nxt, dp)),
        send(planes.at[5:9], planes.at[9:13], halo_send.at[1], halo_recv.at[1], (prv, dp)),
        send(planes.at[8], planes.at[0], halo_send.at[2], halo_recv.at[2], (nxt2, dp)),
        send(planes.at[5], planes.at[13], halo_send.at[3], halo_recv.at[3], (prv2, dp)),
        send(cots.at[1], cotr.at[0], halo_send.at[4], halo_recv.at[4], (nxt, dp)),
        send(cots.at[0], cotr.at[1], halo_send.at[5], halo_recv.at[5], (prv, dp)),
    ]

    k = iota((1, 224), 1)
    m = k % 48
    odd = jnp.logical_and(m >= 24, k < 192)
    v_k = (k // 48) * 2 + jnp.where(odd, 1, 0)
    p_k = jnp.where(odd, jnp.where(m < 32, m // 4 - 2, m // 4 - 8), m // 4)
    for d in range(4):
        kd = p_k - d
        ok = jnp.logical_and(kd >= 0, kd <= 2)
        target = jnp.where(ok, (k % 4) * 27 + kd * 9 + v_k, -1)
        tsel[d] = jnp.where(iota((128, 224), 0) == target, 1.0, 0.0).astype(BF16)
    w1rows[...] = jnp.zeros((128, 128), F32)
    loads[2].wait()
    for t in range(27):
        w1rows[pl.ds(t, 4, stride=27), 0:32] = w1[t].astype(F32)
    w1t = w1rows[...].T[0:32].astype(BF16)
    for d in range(4):
        w1big[d * 32:(d + 1) * 32, :] = (0.5 * dot(w1t, tsel[d])).astype(BF16)

    for blk in range(4):
        r = iota((256, 256), 0) + blk * 256
        pool[blk * 256:(blk + 1) * 256, :] = jnp.where(
            iota((256, 256), 1) == (r // 64) * 16 + (r % 32) // 2, 1.0, 0.0
        ).astype(BF16)

    loads[3].wait()
    zero = jnp.zeros((32, 64), F32)
    for v in range(9):
        w = [w2[kd * 9 + v].astype(F32) for kd in range(3)]
        left = jnp.concatenate([w[0], w[1], w[2], zero], axis=0)
        right = jnp.concatenate([zero, w[0], w[1], w[2]], axis=0)
        both = jnp.concatenate([left, right], axis=1)
        w2band[:, v * 128:(v + 1) * 128] = (0.5 * both.T).astype(BF16)
        top = jnp.concatenate([w[2], w[1], w[0], zero], axis=1)
        bottom = jnp.concatenate([zero, w[2], w[1], w[0]], axis=1)
        wp[v * 64:v * 64 + 32, :] = top.astype(BF16)
        wp[v * 64 + 32:v * 64 + 64, :] = bottom.astype(BF16)

    for copy in halos[0:4]:
        copy.wait_recv()
    first, last = space == 0, space == slabs - 1
    row = iota((64, 1), 0) // 4
    inside = jnp.logical_and(row >= 5 - 4 * space, row < 5 + 4 * (slabs - space))
    field = jnp.where(inside, planes[...].reshape(64, 1024).astype(F32), 0.0).astype(BF16)
    masks_one = tap_masks(32)
    blocks = []
    for v in range(9):
        blocks.append(shifted(field, v, masks_one, 32))
        if v % 2 == 0 and v < 8:
            continue
        for g in range(3):
            top, mid, low = g * 16, g * 16 + 16, g * 16 + 24
            if v == 8:
                x1[g, 192:224, :] = blocks[8][top:top + 32]
                continue
            base = (v // 2) * 48
            x1[g, base:base + 16, :] = blocks[v - 1][top:mid]
            x1[g, base + 16:base + 32, :] = jnp.concatenate(
                [blocks[v - 1][mid:low], blocks[v][mid:low]], axis=0
            )
            x1[g, base + 32:base + 48, :] = blocks[v][top:mid]
    masks = tap_masks(16)
    for g in (0, 2, 1):
        sums = None
        for n in range(4):
            lanes = slice(n * 256, (n + 1) * 256)
            act, s = silu_parts(dot(w1big[...], x1[g, :, lanes]))
            if g == 1:
                dsilu_one[:, lanes] = s + act * (1.0 - s)
            total = jnp.concatenate([act[0:32] + act[32:64], act[64:96] + act[96:128]], axis=0)
            high = total.astype(BF16)
            low = (total - high.astype(F32)).astype(BF16)
            part = dot(jnp.concatenate([high, low], axis=0), pool[lanes, :])
            sums = part if sums is None else sums + part
        pooled = (sums[0:64] + sums[64:128]) * 0.125
        if g == 0:
            pooled = jnp.where(first, 0.0, pooled)
        if g == 2:
            pooled = jnp.where(last, 0.0, pooled)
        pooled = pooled.astype(BF16)
        for v in range(9):
            block = shifted(pooled, v, masks, 16)
            if g < 2:
                xcol_a[v * 128 + g * 64:v * 128 + g * 64 + 64, :] = block
            if g > 0:
                xcol_b[v * 128 + g * 64 - 64:v * 128 + g * 64, :] = block

    halos[4].wait_recv()
    halos[5].wait_recv()
    cot_a = jnp.concatenate([cotr[0].astype(F32), cots[0].astype(F32)], axis=0)
    cot_b = jnp.concatenate([cots[1].astype(F32), cotr[1].astype(F32)], axis=0)
    act_a, s_a = silu_parts(dot(w2band[...], xcol_a[...]))
    delta_a = cot_a * (s_a + act_a * (1.0 - s_a))
    act_b, s_b = silu_parts(dot(w2band[...], xcol_b[...]))
    delta_b = cot_b * (s_b + act_b * (1.0 - s_b))
    delta = jnp.concatenate(
        [
            jnp.where(first, 0.0, delta_a[0:64]),
            delta_a[64:128],
            delta_b[0:64],
            jnp.where(last, 0.0, delta_b[64:128]),
        ],
        axis=0,
    ).astype(BF16)

    rows_xy, rows_z = 64 // tiles_n, 64 // slabs
    scale_two = 1.0 / 512.0 * math.sqrt(64 * 8 / (slabs * dp_n))
    lower = dot_nt(delta[64:128], xcol_a[...])
    upper = dot_nt(delta[128:192], xcol_b[...])
    tiles = []
    for v in range(9):
        lanes = slice(v * 128, (v + 1) * 128)
        tiles.append(pltpu.roll(lower[:, lanes], 96, 1) + upper[:, lanes])
    lane = iota((1, 128), 1)
    for v in range(7):
        tile = tiles[v]
        if v < 6:
            kd = v % 3
            tile = jnp.where(lane < 96, tile, pltpu.roll(tiles[7 + v // 3], 96 - kd * 32, 1))
        g2s[:, :, v * 128:(v + 1) * 128] = (tile * scale_two).astype(BF16).reshape(tiles_n, rows_xy, 128)
    g2_x = []
    for r in range(1, tiles_n):
        other, peer = xy_peer(r)
        g2_x.append(send(g2s.at[other], g2x.at[xy], xs.at[0, r - 1], xr.at[0, xy], peer))
    for copy in halos:
        copy.wait_send()

    z = dot(wp[...], delta)
    total = None
    for v in range(9):
        term = shifted(z[v * 64:(v + 1) * 64], v, masks, 16, sign=-1)
        total = term if total is None else total + term
    pg = total.astype(BF16)

    g1k = None
    for n in range(4):
        lanes = slice(n * 256, (n + 1) * 256)
        spread = dot_nt(pg, pool[lanes, :]) * 0.125
        twice = jnp.concatenate([spread[0:32], spread[0:32], spread[32:64], spread[32:64]], axis=0)
        one = (twice * dsilu_one[:, lanes]).astype(BF16)
        part = dot_nt(one, x1[1, :, lanes])
        g1k = part if g1k is None else g1k + part
    hi = g1k.astype(BF16)
    mid = (g1k - hi.astype(F32)).astype(BF16)
    g1 = None
    for d in range(4):
        rows = slice(d * 32, (d + 1) * 32)
        out = dot_nt(jnp.concatenate([hi[rows], mid[rows]], axis=0), tsel[d])
        g1 = out if g1 is None else g1 + out
    g1 = (g1[0:32] + g1[32:64]) * (1.0 / math.sqrt(4096 * slabs * dp_n))
    q_y = 32 // tiles_n
    g1s[...] = g1.reshape(tiles_n, q_y, 128)
    g1_x = []
    for r in range(1, tiles_n):
        other, peer = xy_peer(r)
        g1_x.append(send(g1s.at[other], g1x.at[xy], xs.at[1, r - 1], xr.at[1, xy], peer))
    g2x[xy] = g2s[xy]
    g1x[xy] = g1s[xy]

    own_feat = jnp.concatenate([act_a[64:128], act_b[0:64]], axis=0).astype(BF16)
    feat[...] = dot(merge, own_feat).astype(BF16).reshape(64, 2, 256)
    pgrad[...] = dot(merge_half, pg).astype(BF16).reshape(32, 2, 256)

    f = iota((1, 896), 1)
    f_v, f_kd, f_c = f % 9, (f % 27) // 9, f // 27
    f_row = jnp.where(f_v < 7, f_v, (f_v - 7) * 3 + f_kd)
    f_lane = jnp.where(f < 864, jnp.where(f_v < 7, f_kd * 32 + f_c, 96 + f_c), -1)
    place[...] = jnp.where(iota((128, 896), 0) == f_lane, 1.0, 0.0).astype(BF16)

    for r in range(1, tiles_n):
        other, peer = xy_peer(r)
        g2_x[r - 1].wait_send()
        pltpu.make_async_remote_copy(
            src_ref=g2s.at[xy], dst_ref=g2x.at[other], send_sem=xs.at[0, r - 1],
            recv_sem=xr.at[0, other], device_id=peer, device_id_type=pl.DeviceIdType.MESH,
        ).wait_recv()
    parts = g2x[...].reshape(64, cols).astype(F32)
    step = 64
    while step > max(rows_xy, 8):
        step //= 2
        parts = parts[0:step] + parts[step:2 * step]
    total = parts[0:rows_xy]
    for i in range(1, step // rows_xy):
        total = total + parts[i * rows_xy:(i + 1) * rows_xy]
    for i in range(nz):
        rows = []
        for q in range(i * rows_z, (i + 1) * rows_z):
            rows += [total[q:q + 1, v * 128:(v + 1) * 128] for v in range(7)] + [jnp.zeros((1, 128), F32)]
        g2z[i] = jnp.concatenate(rows, axis=0).astype(BF16)
    g2r[me_z] = g2z[zl]
    g2_z = []
    for r in range(1, team):
        other, oz, peer = z_peer(r)
        g2_z.append(send(g2z.at[oz], g2r.at[me_z], zs.at[0, r - 1], zr.at[0, me_z], peer))

    for r in range(1, tiles_n):
        other, peer = xy_peer(r)
        g1_x[r - 1].wait_send()
        pltpu.make_async_remote_copy(
            src_ref=g1s.at[xy], dst_ref=g1x.at[other], send_sem=xs.at[1, r - 1],
            recv_sem=xr.at[1, other], device_id=peer, device_id_type=pl.DeviceIdType.MESH,
        ).wait_recv()
    parts = g1x[...].reshape(32, 128)
    step = 32
    while step > max(q_y, 8):
        step //= 2
        parts = parts[0:step] + parts[step:2 * step]
    total = parts[0:q_y]
    for i in range(1, step // q_y):
        total = total + parts[i * q_y:(i + 1) * q_y]
    g1z[...] = total
    g1r[me_z] = total
    g1_z = []
    for r in range(1, team):
        other, oz, peer = z_peer(r)
        g1_z.append(send(g1z, g1r.at[me_z], zs.at[1, r - 1], zr.at[1, me_z], peer))

    for r in range(1, team):
        other, oz, peer = z_peer(r)
        g2_z[r - 1].wait_send()
        pltpu.make_async_remote_copy(
            src_ref=g2z.at[zl], dst_ref=g2r.at[other], send_sem=zs.at[0, r - 1],
            recv_sem=zr.at[0, other], device_id=peer, device_id_type=pl.DeviceIdType.MESH,
        ).wait_recv()
    total = g2r[0].astype(F32)
    for r in range(1, team):
        total = total + g2r[r].astype(F32)
    for q in range(rows_z):
        packed = total[q * 8:q * 8 + 8]
        hi = packed.astype(BF16)
        rest = packed - hi.astype(F32)
        mid = rest.astype(BF16)
        low = (rest - mid.astype(F32)).astype(BF16)
        split3 = jnp.concatenate([hi.astype(F32), mid.astype(F32), low.astype(F32)], axis=0)
        spread = dot(split3.astype(BF16), place[...])
        spread = spread[0:8] + (spread[8:16] + spread[16:24])
        spread = jnp.where(iota((8, 896), 0) == f_row, spread, 0.0)
        g2_out[q:q + 1, :] = jnp.sum(spread, axis=0, keepdims=True)
    for r in range(1, team):
        other, oz, peer = z_peer(r)
        g1_z[r - 1].wait_send()
        pltpu.make_async_remote_copy(
            src_ref=g1z, dst_ref=g1r.at[other], send_sem=zs.at[1, r - 1],
            recv_sem=zr.at[1, other], device_id=peer, device_id_type=pl.DeviceIdType.MESH,
        ).wait_recv()
    total = g1r[0]
    for r in range(1, team):
        total = total + g1r[r]
    if q_y == 1:
        total = jnp.where(zl == 0, total, pltpu.roll(total, 128 - 54, 1))
    g1_out[...] = total


def finish(feat, pgrad, g1, g2, feat_out, pgrad_out, g1_out, g2_out, one, two, sems):
    copies = [
        pltpu.make_async_copy(feat, feat_out, sems.at[0]),
        pltpu.make_async_copy(pgrad, pgrad_out, sems.at[1]),
    ]
    for copy in copies:
        copy.start()
    one[...] = g1[0, 0:54]
    two[...] = g2[0, 0:864]
    tails = [
        pltpu.make_async_copy(one, g1_out, sems.at[2]),
        pltpu.make_async_copy(two, g2_out, sems.at[3]),
    ]
    for copy in tails:
        copy.start()
    for copy in copies + tails:
        copy.wait()


def on_device(sizes, volumes, kernel_one, kernel_two, cotangent):
    nx, ny, nz, dp_n = sizes
    slabs, team = nx * ny * nz, nz * dp_n
    w1 = jnp.transpose(kernel_one, (2, 3, 4, 1, 0)).reshape(27, 4, 32)
    w2 = jnp.transpose(kernel_two, (2, 3, 4, 1, 0)).reshape(27, 32, 64)
    tiles_n = nx * ny
    rows_xy, rows_z, q_y = 64 // tiles_n, 64 // slabs, 32 // tiles_n
    cols = 896
    vmem = pl.BlockSpec(memory_space=pltpu.VMEM)
    hbm = pl.BlockSpec(memory_space=pltpu.HBM)
    scratch = [
        ((4, 4, 32, 32), BF16),
        ((27, 4, 32), BF16),
        ((27, 32, 64), BF16),
        ((64, 2, 256), BF16),
        ((512, 32), F32),
        ((16, 4, 1024), BF16),
        ((2, 64, 256), BF16),
        ((2, 64, 256), BF16),
        ((128, 128), F32),
        ((3, 224, 1024), BF16),
        ((4, 128, 224), BF16),
        ((128, 224), BF16),
        ((1024, 256), BF16),
        ((128, 1024), F32),
        ((128, 1152), BF16),
        ((576, 256), BF16),
        ((128, cols), BF16),
        ((1152, 256), BF16),
        ((1152, 256), BF16),
        ((tiles_n, rows_xy, cols), BF16),
        ((tiles_n, rows_xy, cols), BF16),
        ((nz, rows_z * 8, 128), BF16),
        ((team, rows_z * 8, 128), BF16),
        ((tiles_n, q_y, 128), F32),
        ((tiles_n, q_y, 128), F32),
        ((q_y, 128), F32),
        ((team, q_y, 128), F32),
    ]
    dma = pltpu.SemaphoreType.DMA
    features, pooled_grad, g1, g2 = pl.pallas_call(
        functools.partial(kernel, sizes, cols),
        out_shape=(
            jax.ShapeDtypeStruct((64, 2, 256), BF16),
            jax.ShapeDtypeStruct((32, 2, 256), BF16),
            jax.ShapeDtypeStruct((q_y, 128), F32),
            jax.ShapeDtypeStruct((rows_z, cols), F32),
        ),
        in_specs=[hbm] * 4,
        out_specs=(vmem,) * 4,
        scratch_shapes=[pltpu.VMEM(shape, dtype) for shape, dtype in scratch] + [
            dma((4,)), dma((6,)), dma((6,)),
            dma((2, tiles_n - 1)), dma((2, tiles_n)),
            dma((2, team - 1)), dma((2, team)),
        ],
        compiler_params=pltpu.CompilerParams(
            collective_id=0, has_side_effects=True, vmem_limit_bytes=24 * 2**20
        ),
        name="conv_step",
    )(*(pltpu.with_memory_space_constraint(a, pltpu.HBM) for a in (volumes[0], w1, w2, cotangent[0])))
    if q_y > 1:
        half = q_y * 108 // nz
        zl = lax.rem(lax.axis_index("space"), nz)
        grad_one = lax.dynamic_slice_in_dim(g1[:, :108].reshape(-1), zl * half, half, 0)
        return features[None], pooled_grad[None], grad_one, g2[:, :864].reshape(-1)
    features, pooled_grad, grad_one, grad_two = pl.pallas_call(
        finish,
        out_shape=(
            jax.ShapeDtypeStruct((64, 2, 256), BF16),
            jax.ShapeDtypeStruct((32, 2, 256), BF16),
            jax.ShapeDtypeStruct((54,), F32),
            jax.ShapeDtypeStruct((864,), F32),
        ),
        in_specs=[vmem] * 4,
        out_specs=(hbm,) * 4,
        scratch_shapes=[pltpu.VMEM((54,), F32), pltpu.VMEM((864,), F32), dma((4,))],
        compiler_params=pltpu.CompilerParams(vmem_limit_bytes=2 * 2**20),
        name="finish",
    )(features, pooled_grad, g1, g2)
    return features[None], pooled_grad[None], grad_one, grad_two


def solution(mesh):
    slabs, dp_n = mesh.shape["space"], mesh.shape["dp"]
    sizes = (4, 8, 2, dp_n) if slabs == 64 else (2, 2, slabs // 4, dp_n)
    in_specs = (P("dp", None, "space", None, None), P(), P(), P("dp", None, "space", None))
    out_specs = (P("dp", None, "space", None), P("dp", None, "space", None), P("space"), P("space"))
    return jax.shard_map(
        functools.partial(on_device, sizes), mesh=mesh, in_specs=in_specs, out_specs=out_specs,
        check_vma=False,
    )
```

time: 43 us -> 37 us (0.86)
  local copies, waits for them, and re-layouts: 3.68 us -> 0 us
  Pallas kernels: 38.4 us -> 36.2 us
    unnamed x11 -> x0, local copies, waits for them, and re-layouts: 2.24 us -> none
    pallas_call x1 -> x2, Pallas kernels: 38.4 us -> 36.2 us  [the longest x1 35.5 us: on_device(): pl.pallas_call(functools.partial(kernel, sizes, cols), out_shape=(jax.Sha...]
    reshape x2 -> x0, local copies, waits for them, and re-layouts: 0.86 us -> none  [the longest x1 0.77 us: on_device(): jnp.transpose(g2.reshape(rows_z, 9, 4, 32)[:, :, :3], (0, 3, 2, 1))]
    dynamic_slice x1 -> x0, local copies, waits for them, and re-layouts: 0.58 us -> none  [on_device(): grad_one = lax.dynamic_slice_in_dim(flat_one, zl * half, half, 0)]
where the time goes in v3:
time: 37 us; the launch traced here: 36.8 us
  Pallas kernels  36.2 us (98%)
  between operations  0.64 us (2%)
    pallas_call x1, Pallas kernels, on_device(): pl.pallas_call(functools.partial(kernel, sizes, cols), out_shape=(jax.Sha...  35.5 us

profile of v3, /device:TPU:1, one launch (start us, length us, event | category | flops | bytes accessed | tf_op | source)
XLA Modules:
  0.0 36.8 jit_solution(10925857053093927281)
XLA Ops:
  0.6 35.5 %conv_step.1 = (bf16[64,2,256]{2,1,0:T(2,128)(2,1)S(1)}, bf16[32,2,256]{2,1,0:T(2,128)(2,1)S(1)}, f32[1,128]{1,0:T(1,128)S(1)}, f32[1,896]{1,0:T(1,128)S(1)}) custom-call(bf16[4,4,32,32]{3,2,1,0:T(8,128)(2,1)} %bitcast.11, bf16[27,4,32]{2,1,0:T(4,128)(2,1)} %bitcast.13, bf16[27,32,64]{2,1,0:T(8,128)(2,1)} %bitcast.10, bf16[64,2,256]{2,1,0:T(2,128)(2,1)} %bitcast.12), custom_call_target="tpu_custom_call" | custom-call | tf_op jit(solution)/shard_map/conv_step/pallas_call | solution.py:461
  36.2 0.7 %finish.1 = (bf16[64,2,256]{2,1,0:T(2,128)(2,1)}, bf16[32,2,256]{2,1,0:T(2,128)(2,1)}, f32[54]{0:T(128)}, f32[864]{0:T(1024)}) custom-call(bf16[64,2,256]{2,1,0:T(2,128)(2,1)S(1)} %get-tuple-element.12.feat, bf16[32,2,256]{2,1,0:T(2,128)(2,1)S(1)} %get-tuple-element.13.pgrad, f32[1,128]{1,0:T(1,128)S(1)} %get-tuple-element.14.g1, ...), custom_call_target="tpu_custom_call" | custom-call | tf_op jit(solution)/shard_map/finish/pallas_call | solution.py:486

commit v4 on v3

--- a/solution.py
+++ b/solution.py
@@ -70,7 +70,7 @@
     xcol_a, xcol_b,
     g2s, g2x, g2z, g2r,
     g1s, g1x, g1z, g1r,
-    local, halo_send, halo_recv, xs, xr, zs, zr,
+    local, halo_send, halo_recv, xs, xr, zs, zr, news,
 ):
     nx, ny, nz, dp_n = sizes
     slabs = nx * ny * nz
@@ -86,14 +86,51 @@
     team = nz * dp_n
     me_z = zl * dp_n + dp
 
+    yi = lax.rem(xy, ny)
+    xi = lax.div(xy, ny)
+    core = lax.rem(dp, 2)
+    ring_z = nz * dp_n // 2
+    zi = lax.div(dp, 2) * nz + zl
+
+    def at(dx, dy, dz, dc):
+        ox, oy = lax.rem(xi + dx % nx, nx), lax.rem(yi + dy % ny, ny)
+        oz, oc = lax.rem(zi + dz % ring_z, ring_z), lax.rem(core + dc, 2)
+        return (ox * ny + oy) * nz + lax.rem(oz, nz), lax.div(oz, nz) * 2 + oc
+
+    def around(d, n):
+        return min(d, n - d)
+
+    xy_offsets = sorted(
+        ((dx, dy) for dx in range(nx) for dy in range(ny) if dx or dy),
+        key=lambda o: -around(o[0], nx) - around(o[1], ny),
+    )
+    z_offsets = sorted(
+        ((dz, dc) for dz in range(ring_z) for dc in range(2) if dz or dc),
+        key=lambda o: -around(o[0], ring_z) - 0.5 * o[1],
+    )
+
     def xy_peer(r):
-        other = lax.rem(xy + r, tiles_n)
-        return other, (other * nz + zl, dp)
+        dx, dy = xy_offsets[r - 1]
+        peer = at(dx, dy, 0, 0)
+        return lax.div(peer[0], nz), peer
 
     def z_peer(r):
-        other = lax.rem(me_z + r, team)
-        oz = lax.div(other, dp_n)
-        return other, oz, (xy * nz + oz, lax.rem(other, dp_n))
+        dz, dc = z_offsets[r - 1]
+        peer = at(0, 0, dz, dc)
+        oz = lax.rem(peer[0], nz)
+        return oz * dp_n + peer[1], oz, peer
+
+    def signal(sem, where):
+        for peer in where:
+            pl.semaphore_signal(sem, inc=1, device_id=peer, device_id_type=pl.DeviceIdType.MESH)
+
+    near = [at(0, 0, 0, 1)]
+    near += [at(d, 0, 0, 0) for d in (-1, 1)] + [at(0, d, 0, 0) for d in (-1, 1)]
+    near += [at(0, 0, d, 0) for d in (-1, 1)]
+    wide = [at(2, 0, 0, 0)] if nx > 2 else []
+    wide += [at(0, d, 0, 0) for d in (-2, 2)] if ny > 2 else []
+    wide += [at(0, 0, d, 0) for d in (-2, 2)] if ring_z > 2 else []
+    widest = ([at(0, d, 0, 0) for d in (-2, 2)] if ny > 2 else []) + [at(0, 0, 0, 1)]
 
     loads = [
         pltpu.make_async_copy(src, dst, local.at[i])
@@ -102,11 +139,8 @@
     for copy in loads:
         copy.start()
     barrier = pltpu.get_barrier_semaphore()
-    peers = [(nxt, dp), (prv, dp), (nxt2, dp), (prv2, dp)]
-    peers += [xy_peer(r)[1] for r in range(1, tiles_n)]
-    peers += [z_peer(r)[2] for r in range(1, team)]
-    for peer in peers:
-        pl.semaphore_signal(barrier, inc=1, device_id=peer, device_id_type=pl.DeviceIdType.MESH)
+    entry = [(nxt, dp), (prv, dp), (nxt2, dp), (prv2, dp)] + near
+    signal(barrier, entry)
 
     def send(src, dst, ssem, rsem, peer):
         copy = pltpu.make_async_remote_copy(
@@ -137,7 +171,7 @@
     cots[0] = own_cot[0:64].astype(BF16)
     cots[1] = own_cot[64:128].astype(BF16)
 
-    pl.semaphore_wait(barrier, len(peers))
+    pl.semaphore_wait(barrier, len(entry))
     halos = [
         send(planes.at[5:9], planes.at[1:5], halo_send.at[0], halo_recv.at[0], (nxt, dp)),
         send(planes.at[5:9], planes.at[9:13], halo_send.at[1], halo_recv.at[1], (prv, dp)),
@@ -146,6 +180,8 @@
         send(cots.at[1], cotr.at[0], halo_send.at[4], halo_recv.at[4], (nxt, dp)),
         send(cots.at[0], cotr.at[1], halo_send.at[5], halo_recv.at[5], (prv, dp)),
     ]
+
+    signal(news.at[0], near)
 
     k = iota((1, 224), 1)
     m = k % 48
@@ -165,6 +201,8 @@
     for d in range(4):
         w1big[d * 32:(d + 1) * 32, :] = (0.5 * dot(w1t, tsel[d])).astype(BF16)
 
+    pl.semaphore_wait(news.at[0], len(near))
+    signal(news.at[1], wide)
     for blk in range(4):
         r = iota((256, 256), 0) + blk * 256
         pool[blk * 256:(blk + 1) * 256, :] = jnp.where(
@@ -184,6 +222,9 @@
         wp[v * 64:v * 64 + 32, :] = top.astype(BF16)
         wp[v * 64 + 32:v * 64 + 64, :] = bottom.astype(BF16)
 
+    if wide:
+        pl.semaphore_wait(news.at[1], len(wide))
+    signal(news.at[2], widest)
     for copy in halos[0:4]:
         copy.wait_recv()
     first, last = space == 0, space == slabs - 1
@@ -266,6 +307,7 @@
             kd = v % 3
             tile = jnp.where(lane < 96, tile, pltpu.roll(tiles[7 + v // 3], 96 - kd * 32, 1))
         g2s[:, :, v * 128:(v + 1) * 128] = (tile * scale_two).astype(BF16).reshape(tiles_n, rows_xy, 128)
+    pl.semaphore_wait(news.at[2], len(widest))
     g2_x = []
     for r in range(1, tiles_n):
         other, peer = xy_peer(r)
@@ -472,6 +514,7 @@
             dma((4,)), dma((6,)), dma((6,)),
             dma((2, tiles_n - 1)), dma((2, tiles_n)),
             dma((2, team - 1)), dma((2, team)),
+            pltpu.SemaphoreType.REGULAR((3,)),
         ],
         compiler_params=pltpu.CompilerParams(
             collective_id=0, has_side_effects=True, vmem_limit_bytes=24 * 2**20

time: 37 us -> 35.1 us (0.949)
  Pallas kernels: 36.2 us -> 34.3 us
    pallas_call x1, Pallas kernels: 35.5 us -> 33.6 us  [on_device(): pl.pallas_call(functools.partial(kernel, sizes, cols), out_shape=(jax.Sha...]
where the time goes in v4:
time: 35.1 us; the launch traced here: 34.9 us
  Pallas kernels  34.3 us (98%)
  between operations  0.64 us (2%)
    pallas_call x1, Pallas kernels, on_device(): pl.pallas_call(functools.partial(kernel, sizes, cols), out_shape=(jax.Sha...  33.6 us

profile of v4, /device:TPU:1, one launch (start us, length us, event | category | flops | bytes accessed | tf_op | source)
XLA Modules:
  0.0 34.9 jit_solution(3940707873365636748)
XLA Ops:
  0.6 33.6 %conv_step.1 = (bf16[64,2,256]{2,1,0:T(2,128)(2,1)S(1)}, bf16[32,2,256]{2,1,0:T(2,128)(2,1)S(1)}, f32[1,128]{1,0:T(1,128)S(1)}, f32[1,896]{1,0:T(1,128)S(1)}) custom-call(bf16[4,4,32,32]{3,2,1,0:T(8,128)(2,1)} %bitcast.11, bf16[27,4,32]{2,1,0:T(4,128)(2,1)} %bitcast.13, bf16[27,32,64]{2,1,0:T(8,128)(2,1)} %bitcast.10, bf16[64,2,256]{2,1,0:T(2,128)(2,1)} %bitcast.12), custom_call_target="tpu_custom_call" | custom-call | tf_op jit(solution)/shard_map/conv_step/pallas_call | solution.py:503
  34.3 0.7 %finish.1 = (bf16[64,2,256]{2,1,0:T(2,128)(2,1)}, bf16[32,2,256]{2,1,0:T(2,128)(2,1)}, f32[54]{0:T(128)}, f32[864]{0:T(1024)}) custom-call(bf16[64,2,256]{2,1,0:T(2,128)(2,1)S(1)} %get-tuple-element.12.feat, bf16[32,2,256]{2,1,0:T(2,128)(2,1)S(1)} %get-tuple-element.13.pgrad, f32[1,128]{1,0:T(1,128)S(1)} %get-tuple-element.14.g1, ...), custom_call_target="tpu_custom_call" | custom-call | tf_op jit(solution)/shard_map/finish/pallas_call | solution.py:529

commit v5 on v4

--- a/solution.py
+++ b/solution.py
@@ -68,8 +68,7 @@
     vrows, planes, cots, cotr, w1rows,
     x1, tsel, w1big, pool, dsilu_one, w2band, wp, place,
     xcol_a, xcol_b,
-    g2s, g2x, g2z, g2r,
-    g1s, g1x, g1z, g1r,
+    g2s, g2x, g1s, g1x, gz, gr,
     local, halo_send, halo_recv, xs, xr, zs, zr, news,
 ):
     nx, ny, nz, dp_n = sizes
@@ -125,20 +124,18 @@
             pl.semaphore_signal(sem, inc=1, device_id=peer, device_id_type=pl.DeviceIdType.MESH)
 
     near = [at(0, 0, 0, 1)]
-    near += [at(d, 0, 0, 0) for d in (-1, 1)] + [at(0, d, 0, 0) for d in (-1, 1)]
-    near += [at(0, 0, d, 0) for d in (-1, 1)]
-    wide = [at(2, 0, 0, 0)] if nx > 2 else []
-    wide += [at(0, d, 0, 0) for d in (-2, 2)] if ny > 2 else []
-    wide += [at(0, 0, d, 0) for d in (-2, 2)] if ring_z > 2 else []
-    widest = ([at(0, d, 0, 0) for d in (-2, 2)] if ny > 2 else []) + [at(0, 0, 0, 1)]
-
+    near += [at(d, 0, 0, 0) for d in range(1, nx)]
+    near += [at(0, d, 0, 0) for d in (-2, -1, 1, 2) if ny > 2 or abs(d) == 1]
+    near += [at(0, 0, d, 0) for d in (-2, -1, 1, 2) if ring_z > 2 or abs(d) == 1]
+    wide = [at(d, 0, 0, 0) for d in range(1, nx)] + [at(0, 0, 0, 1)]
+
+    barrier = pltpu.get_barrier_semaphore()
     loads = [
         pltpu.make_async_copy(src, dst, local.at[i])
         for i, (src, dst) in enumerate([(vol_in, vol), (cot_in, cot), (w1_in, w1), (w2_in, w2)])
     ]
     for copy in loads:
         copy.start()
-    barrier = pltpu.get_barrier_semaphore()
     entry = [(nxt, dp), (prv, dp), (nxt2, dp), (prv2, dp)] + near
     signal(barrier, entry)
 
@@ -222,9 +219,6 @@
         wp[v * 64:v * 64 + 32, :] = top.astype(BF16)
         wp[v * 64 + 32:v * 64 + 64, :] = bottom.astype(BF16)
 
-    if wide:
-        pl.semaphore_wait(news.at[1], len(wide))
-    signal(news.at[2], widest)
     for copy in halos[0:4]:
         copy.wait_recv()
     first, last = space == 0, space == slabs - 1
@@ -307,11 +301,10 @@
             kd = v % 3
             tile = jnp.where(lane < 96, tile, pltpu.roll(tiles[7 + v // 3], 96 - kd * 32, 1))
         g2s[:, :, v * 128:(v + 1) * 128] = (tile * scale_two).astype(BF16).reshape(tiles_n, rows_xy, 128)
-    pl.semaphore_wait(news.at[2], len(widest))
-    g2_x = []
+    pl.semaphore_wait(news.at[1], len(wide))
     for r in range(1, tiles_n):
         other, peer = xy_peer(r)
-        g2_x.append(send(g2s.at[other], g2x.at[xy], xs.at[0, r - 1], xr.at[0, xy], peer))
+        send(g2s.at[other], g2x.at[xy], xs.at[0], xr.at[0], peer)
     for copy in halos:
         copy.wait_send()
 
@@ -340,10 +333,9 @@
     g1 = (g1[0:32] + g1[32:64]) * (1.0 / math.sqrt(4096 * slabs * dp_n))
     q_y = 32 // tiles_n
     g1s[...] = g1.reshape(tiles_n, q_y, 128)
-    g1_x = []
     for r in range(1, tiles_n):
         other, peer = xy_peer(r)
-        g1_x.append(send(g1s.at[other], g1x.at[xy], xs.at[1, r - 1], xr.at[1, xy], peer))
+        send(g1s.at[other], g1x.at[xy], xs.at[1], xr.at[1], peer)
     g2x[xy] = g2s[xy]
     g1x[xy] = g1s[xy]
 
@@ -357,64 +349,47 @@
     f_lane = jnp.where(f < 864, jnp.where(f_v < 7, f_kd * 32 + f_c, 96 + f_c), -1)
     place[...] = jnp.where(iota((128, 896), 0) == f_lane, 1.0, 0.0).astype(BF16)
 
-    for r in range(1, tiles_n):
-        other, peer = xy_peer(r)
-        g2_x[r - 1].wait_send()
-        pltpu.make_async_remote_copy(
-            src_ref=g2s.at[xy], dst_ref=g2x.at[other], send_sem=xs.at[0, r - 1],
-            recv_sem=xr.at[0, other], device_id=peer, device_id_type=pl.DeviceIdType.MESH,
-        ).wait_recv()
-    parts = g2x[...].reshape(64, cols).astype(F32)
-    step = 64
-    while step > max(rows_xy, 8):
-        step //= 2
-        parts = parts[0:step] + parts[step:2 * step]
-    total = parts[0:rows_xy]
-    for i in range(1, step // rows_xy):
-        total = total + parts[i * rows_xy:(i + 1) * rows_xy]
+    def whole(src, dst, count, ssem, rsem):
+        return pltpu.make_async_remote_copy(
+            src_ref=src.at[0:count], dst_ref=dst.at[0:count], send_sem=ssem, recv_sem=rsem,
+            device_id=at(1, 0, 0, 0), device_id_type=pl.DeviceIdType.MESH,
+        )
+
+    def fold(parts, rows):
+        step = parts.shape[0]
+        while step > max(rows, 8):
+            step //= 2
+            parts = parts[0:step] + parts[step:2 * step]
+        total = parts[0:rows]
+        for i in range(1, step // rows):
+            total = total + parts[i * rows:(i + 1) * rows]
+        return total
+
+    all_two = whole(g2s, g2x, tiles_n - 1, xs.at[0], xr.at[0])
+    all_one = whole(g1s, g1x, tiles_n - 1, xs.at[1], xr.at[1])
+    all_two.wait_recv()
+    sum_two = fold(g2x[...].reshape(64, cols).astype(F32), rows_xy)
+    all_one.wait_recv()
+    sum_one = fold(g1x[...].reshape(32, 128), q_y)
     for i in range(nz):
         rows = []
-        for q in range(i * rows_z, (i + 1) * rows_z):
-            rows += [total[q:q + 1, v * 128:(v + 1) * 128] for v in range(7)] + [jnp.zeros((1, 128), F32)]
-        g2z[i] = jnp.concatenate(rows, axis=0).astype(BF16)
-    g2r[me_z] = g2z[zl]
-    g2_z = []
+        for q in range(rows_z):
+            at_row = slice(i * rows_z + q, i * rows_z + q + 1)
+            rows += [sum_two[at_row, v * 128:(v + 1) * 128] for v in range(7)] + [sum_one[q:q + 1]]
+        gz[i] = jnp.concatenate(rows, axis=0).astype(BF16)
     for r in range(1, team):
         other, oz, peer = z_peer(r)
-        g2_z.append(send(g2z.at[oz], g2r.at[me_z], zs.at[0, r - 1], zr.at[0, me_z], peer))
-
-    for r in range(1, tiles_n):
-        other, peer = xy_peer(r)
-        g1_x[r - 1].wait_send()
-        pltpu.make_async_remote_copy(
-            src_ref=g1s.at[xy], dst_ref=g1x.at[other], send_sem=xs.at[1, r - 1],
-            recv_sem=xr.at[1, other], device_id=peer, device_id_type=pl.DeviceIdType.MESH,
-        ).wait_recv()
-    parts = g1x[...].reshape(32, 128)
-    step = 32
-    while step > max(q_y, 8):
-        step //= 2
-        parts = parts[0:step] + parts[step:2 * step]
-    total = parts[0:q_y]
-    for i in range(1, step // q_y):
-        total = total + parts[i * q_y:(i + 1) * q_y]
-    g1z[...] = total
-    g1r[me_z] = total
-    g1_z = []
+        send(gz.at[oz], gr.at[me_z], zs.at[0], zr.at[0], peer)
+    gr[me_z] = gz[zl]
+    all_two.wait_send()
+    all_one.wait_send()
+    pltpu.make_async_remote_copy(
+        src_ref=gr.at[0:team - 1], dst_ref=gr.at[0:team - 1], send_sem=zs.at[0], recv_sem=zr.at[0],
+        device_id=at(1, 0, 0, 0), device_id_type=pl.DeviceIdType.MESH,
+    ).wait()
+    total = gr[0].astype(F32)
     for r in range(1, team):
-        other, oz, peer = z_peer(r)
-        g1_z.append(send(g1z, g1r.at[me_z], zs.at[1, r - 1], zr.at[1, me_z], peer))
-
-    for r in range(1, team):
-        other, oz, peer = z_peer(r)
-        g2_z[r - 1].wait_send()
-        pltpu.make_async_remote_copy(
-            src_ref=g2z.at[zl], dst_ref=g2r.at[other], send_sem=zs.at[0, r - 1],
-            recv_sem=zr.at[0, other], device_id=peer, device_id_type=pl.DeviceIdType.MESH,
-        ).wait_recv()
-    total = g2r[0].astype(F32)
-    for r in range(1, team):
-        total = total + g2r[r].astype(F32)
+        total = total + gr[r].astype(F32)
     for q in range(rows_z):
         packed = total[q * 8:q * 8 + 8]
         hi = packed.astype(BF16)
@@ -426,19 +401,10 @@
         spread = spread[0:8] + (spread[8:16] + spread[16:24])
         spread = jnp.where(iota((8, 896), 0) == f_row, spread, 0.0)
         g2_out[q:q + 1, :] = jnp.sum(spread, axis=0, keepdims=True)
-    for r in range(1, team):
-        other, oz, peer = z_peer(r)
-        g1_z[r - 1].wait_send()
-        pltpu.make_async_remote_copy(
-            src_ref=g1z, dst_ref=g1r.at[other], send_sem=zs.at[1, r - 1],
-            recv_sem=zr.at[1, other], device_id=peer, device_id_type=pl.DeviceIdType.MESH,
-        ).wait_recv()
-    total = g1r[0]
-    for r in range(1, team):
-        total = total + g1r[r]
-    if q_y == 1:
-        total = jnp.where(zl == 0, total, pltpu.roll(total, 128 - 54, 1))
-    g1_out[...] = total
+        one = packed[7:8]
+        if rows_z == 1:
+            one = jnp.where(zl == 0, one, pltpu.roll(one, 128 - 54, 1))
+        g1_out[q:q + 1, :] = one
 
 
 def finish(feat, pgrad, g1, g2, feat_out, pgrad_out, g1_out, g2_out, one, two, sems):
@@ -492,12 +458,10 @@
         ((1152, 256), BF16),
         ((tiles_n, rows_xy, cols), BF16),
         ((tiles_n, rows_xy, cols), BF16),
+        ((tiles_n, q_y, 128), F32),
+        ((tiles_n, q_y, 128), F32),
         ((nz, rows_z * 8, 128), BF16),
         ((team, rows_z * 8, 128), BF16),
-        ((tiles_n, q_y, 128), F32),
-        ((tiles_n, q_y, 128), F32),
-        ((q_y, 128), F32),
-        ((team, q_y, 128), F32),
     ]
     dma = pltpu.SemaphoreType.DMA
     features, pooled_grad, g1, g2 = pl.pallas_call(
@@ -512,9 +476,8 @@
         out_specs=(vmem,) * 4,
         scratch_shapes=[pltpu.VMEM(shape, dtype) for shape, dtype in scratch] + [
             dma((4,)), dma((6,)), dma((6,)),
-            dma((2, tiles_n - 1)), dma((2, tiles_n)),
-            dma((2, team - 1)), dma((2, team)),
-            pltpu.SemaphoreType.REGULAR((3,)),
+            dma((2,)), dma((2,)), dma((1,)), dma((1,)),
+            pltpu.SemaphoreType.REGULAR((2,)),
         ],
         compiler_params=pltpu.CompilerParams(
             collective_id=0, has_side_effects=True, vmem_limit_bytes=24 * 2**20

time: 35.1 us -> 34.1 us (0.972)
  Pallas kernels: 34.3 us -> 33.3 us
    pallas_call x1, Pallas kernels: 33.6 us -> 32.6 us  [on_device(): pl.pallas_call(functools.partial(kernel, sizes, cols), out_shape=(jax.Sha...]
where the time goes in v5:
time: 34.1 us; the launch traced here: 33.9 us
  Pallas kernels  33.3 us (98%)
  between operations  0.64 us (2%)
    pallas_call x1, Pallas kernels, on_device(): pl.pallas_call(functools.partial(kernel, sizes, cols), out_shape=(jax.Sha...  32.6 us

profile of v5, /device:TPU:1, one launch (start us, length us, event | category | flops | bytes accessed | tf_op | source)
XLA Modules:
  0.0 33.9 jit_solution(10322286156342546236)
XLA Ops:
  0.6 32.6 %conv_step.1 = (bf16[64,2,256]{2,1,0:T(2,128)(2,1)S(1)}, bf16[32,2,256]{2,1,0:T(2,128)(2,1)S(1)}, f32[1,128]{1,0:T(1,128)S(1)}, f32[1,896]{1,0:T(1,128)S(1)}) custom-call(bf16[4,4,32,32]{3,2,1,0:T(8,128)(2,1)} %bitcast.11, bf16[27,4,32]{2,1,0:T(4,128)(2,1)} %bitcast.13, bf16[27,32,64]{2,1,0:T(8,128)(2,1)} %bitcast.10, bf16[64,2,256]{2,1,0:T(2,128)(2,1)} %bitcast.12), custom_call_target="tpu_custom_call" | custom-call | tf_op jit(solution)/shard_map/conv_step/pallas_call | solution.py:467
  33.3 0.7 %finish.1 = (bf16[64,2,256]{2,1,0:T(2,128)(2,1)}, bf16[32,2,256]{2,1,0:T(2,128)(2,1)}, f32[54]{0:T(128)}, f32[864]{0:T(1024)}) custom-call(bf16[64,2,256]{2,1,0:T(2,128)(2,1)S(1)} %get-tuple-element.12.feat, bf16[32,2,256]{2,1,0:T(2,128)(2,1)S(1)} %get-tuple-element.13.pgrad, f32[1,128]{1,0:T(1,128)S(1)} %get-tuple-element.14.g1, ...), custom_call_target="tpu_custom_call" | custom-call | tf_op jit(solution)/shard_map/finish/pallas_call | solution.py:492

commit v6 on v5

--- a/solution.py
+++ b/solution.py
@@ -55,6 +55,16 @@
     return jnp.where(iota(shape, 1) == column_of_row(iota(shape, 0)), 1.0, 0.0).astype(BF16)
 
 
+def shifted_bf16(block, tap, mask, width):
+    dr, dc = TAPS[tap]
+    if dr == 0 and dc == 0:
+        return block
+    moved = pltpu.roll(block, (-(dr * width + dc)) % (width * width), 1)
+    return jnp.concatenate(
+        [moved[r:r + 16] * mask for r in range(0, block.shape[0], 16)], axis=0
+    )
+
+
 def silu_parts(half):
     t = jnp.tanh(half)
     return half + half * t, 0.5 + 0.5 * t
@@ -66,8 +76,8 @@
     feat, pgrad, g1_out, g2_out,
     vol, w1, w2, cot,
     vrows, planes, cots, cotr, w1rows,
-    x1, tsel, w1big, pool, dsilu_one, w2band, wp, place,
-    xcol_a, xcol_b,
+    ones_one, ones_two, x1, tsel, w1big, pool, dsilu_one, w2band, wp, place,
+    xcol_a, xcol_b, xcol_c,
     g2s, g2x, g1s, g1x, gz, gr,
     local, halo_send, halo_recv, xs, xr, zs, zr, news,
 ):
@@ -160,6 +170,15 @@
     )
     planes[5:9] = own.astype(BF16).reshape(4, 4, 1024)
     planes[14:16] = jnp.zeros((2, 4, 1024), BF16)
+    pl.semaphore_wait(barrier, len(entry))
+    halos = [
+        send(planes.at[5:9], planes.at[1:5], halo_send.at[0], halo_recv.at[0], (nxt, dp)),
+        send(planes.at[5:9], planes.at[9:13], halo_send.at[1], halo_recv.at[1], (prv, dp)),
+        send(planes.at[8], planes.at[0], halo_send.at[2], halo_recv.at[2], (nxt2, dp)),
+        send(planes.at[5], planes.at[13], halo_send.at[3], halo_recv.at[3], (prv2, dp)),
+    ]
+
+    signal(news.at[0], near)
     loads[1].wait()
     split = one_hot((128, 128), lambda r: (r % 64) * 2 + r // 64)
     merge = one_hot((128, 128), lambda r: (r % 2) * 64 + r // 2)
@@ -167,18 +186,10 @@
     own_cot = dot(split, cot[...].reshape(128, 256))
     cots[0] = own_cot[0:64].astype(BF16)
     cots[1] = own_cot[64:128].astype(BF16)
-
-    pl.semaphore_wait(barrier, len(entry))
-    halos = [
-        send(planes.at[5:9], planes.at[1:5], halo_send.at[0], halo_recv.at[0], (nxt, dp)),
-        send(planes.at[5:9], planes.at[9:13], halo_send.at[1], halo_recv.at[1], (prv, dp)),
-        send(planes.at[8], planes.at[0], halo_send.at[2], halo_recv.at[2], (nxt2, dp)),
-        send(planes.at[5], planes.at[13], halo_send.at[3], halo_recv.at[3], (prv2, dp)),
+    halos += [
         send(cots.at[1], cotr.at[0], halo_send.at[4], halo_recv.at[4], (nxt, dp)),
         send(cots.at[0], cotr.at[1], halo_send.at[5], halo_recv.at[5], (prv, dp)),
     ]
-
-    signal(news.at[0], near)
 
     k = iota((1, 224), 1)
     m = k % 48
@@ -206,6 +217,11 @@
             iota((256, 256), 1) == (r // 64) * 16 + (r % 32) // 2, 1.0, 0.0
         ).astype(BF16)
 
+    for ones, width in ((ones_one, 32), (ones_two, 16)):
+        for v, mask in enumerate(tap_masks(width)):
+            if mask is not None:
+                row = jnp.where(mask, 1.0, 0.0)
+                ones[v] = jnp.broadcast_to(row, (16, width * width)).astype(BF16)
     loads[3].wait()
     zero = jnp.zeros((32, 64), F32)
     for v in range(9):
@@ -225,10 +241,9 @@
     row = iota((64, 1), 0) // 4
     inside = jnp.logical_and(row >= 5 - 4 * space, row < 5 + 4 * (slabs - space))
     field = jnp.where(inside, planes[...].reshape(64, 1024).astype(F32), 0.0).astype(BF16)
-    masks_one = tap_masks(32)
     blocks = []
     for v in range(9):
-        blocks.append(shifted(field, v, masks_one, 32))
+        blocks.append(shifted_bf16(field, v, ones_one[v], 32))
         if v % 2 == 0 and v < 8:
             continue
         for g in range(3):
@@ -262,7 +277,13 @@
             pooled = jnp.where(last, 0.0, pooled)
         pooled = pooled.astype(BF16)
         for v in range(9):
-            block = shifted(pooled, v, masks, 16)
+            block = shifted_bf16(pooled, v, ones_two[v], 16)
+            if g == 0:
+                xcol_c[v * 128:v * 128 + 32, :] = block[32:64]
+            if g == 1:
+                xcol_c[v * 128 + 32:v * 128 + 96, :] = block
+            if g == 2:
+                xcol_c[v * 128 + 96:v * 128 + 128, :] = block[0:32]
             if g < 2:
                 xcol_a[v * 128 + g * 64:v * 128 + g * 64 + 64, :] = block
             if g > 0:
@@ -288,12 +309,11 @@
 
     rows_xy, rows_z = 64 // tiles_n, 64 // slabs
     scale_two = 1.0 / 512.0 * math.sqrt(64 * 8 / (slabs * dp_n))
-    lower = dot_nt(delta[64:128], xcol_a[...])
-    upper = dot_nt(delta[128:192], xcol_b[...])
+    outer = dot_nt(delta[64:192], xcol_c[...])
     tiles = []
     for v in range(9):
         lanes = slice(v * 128, (v + 1) * 128)
-        tiles.append(pltpu.roll(lower[:, lanes], 96, 1) + upper[:, lanes])
+        tiles.append(outer[0:64, lanes] + pltpu.roll(outer[64:128, lanes], 96, 1))
     lane = iota((1, 128), 1)
     for v in range(7):
         tile = tiles[v]
@@ -305,15 +325,15 @@
     for r in range(1, tiles_n):
         other, peer = xy_peer(r)
         send(g2s.at[other], g2x.at[xy], xs.at[0], xr.at[0], peer)
-    for copy in halos:
-        copy.wait_send()
-
     z = dot(wp[...], delta)
     total = None
     for v in range(9):
         term = shifted(z[v * 64:(v + 1) * 64], v, masks, 16, sign=-1)
         total = term if total is None else total + term
     pg = total.astype(BF16)
+
+    for copy in halos:
+        copy.wait_send()
 
     g1k = None
     for n in range(4):
@@ -446,6 +466,8 @@
         ((2, 64, 256), BF16),
         ((2, 64, 256), BF16),
         ((128, 128), F32),
+        ((9, 16, 1024), BF16),
+        ((9, 16, 256), BF16),
         ((3, 224, 1024), BF16),
         ((4, 128, 224), BF16),
         ((128, 224), BF16),
@@ -454,6 +476,7 @@
         ((128, 1152), BF16),
         ((576, 256), BF16),
         ((128, cols), BF16),
+        ((1152, 256), BF16),
         ((1152, 256), BF16),
         ((1152, 256), BF16),
         ((tiles_n, rows_xy, cols), BF16),

time: 34.1 us -> 33.9 us (level)
  no operation moved by 1% of the time
where the time goes in v6:
time: 33.9 us; the launch traced here: 33.8 us
  Pallas kernels  33.2 us (98%)
  between operations  0.64 us (2%)
    pallas_call x1, Pallas kernels, on_device(): pl.pallas_call(functools.partial(kernel, sizes, cols), out_shape=(jax.Sha...  32.5 us

profile of v6, /device:TPU:1, one launch (start us, length us, event | category | flops | bytes accessed | tf_op | source)
XLA Modules:
  0.0 33.8 jit_solution(10638503706856750142)
XLA Ops:
  0.6 32.5 %conv_step.1 = (bf16[64,2,256]{2,1,0:T(2,128)(2,1)S(1)}, bf16[32,2,256]{2,1,0:T(2,128)(2,1)S(1)}, f32[1,128]{1,0:T(1,128)S(1)}, f32[1,896]{1,0:T(1,128)S(1)}) custom-call(bf16[4,4,32,32]{3,2,1,0:T(8,128)(2,1)} %bitcast.11, bf16[27,4,32]{2,1,0:T(4,128)(2,1)} %bitcast.13, bf16[27,32,64]{2,1,0:T(8,128)(2,1)} %bitcast.10, bf16[64,2,256]{2,1,0:T(2,128)(2,1)} %bitcast.12), custom_call_target="tpu_custom_call" | custom-call | tf_op jit(solution)/shard_map/conv_step/pallas_call | solution.py:490
  33.1 0.7 %finish.1 = (bf16[64,2,256]{2,1,0:T(2,128)(2,1)}, bf16[32,2,256]{2,1,0:T(2,128)(2,1)}, f32[54]{0:T(128)}, f32[864]{0:T(1024)}) custom-call(bf16[64,2,256]{2,1,0:T(2,128)(2,1)S(1)} %get-tuple-element.12.feat, bf16[32,2,256]{2,1,0:T(2,128)(2,1)S(1)} %get-tuple-element.13.pgrad, f32[1,128]{1,0:T(1,128)S(1)} %get-tuple-element.14.g1, ...), custom_call_target="tpu_custom_call" | custom-call | tf_op jit(solution)/shard_map/finish/pallas_call | solution.py:515

commit v7 on v6

--- a/solution.py
+++ b/solution.py
@@ -289,6 +289,7 @@
             if g > 0:
                 xcol_b[v * 128 + g * 64 - 64:v * 128 + g * 64, :] = block
 
+    pl.semaphore_wait(news.at[1], len(wide))
     halos[4].wait_recv()
     halos[5].wait_recv()
     cot_a = jnp.concatenate([cotr[0].astype(F32), cots[0].astype(F32)], axis=0)
@@ -321,7 +322,6 @@
             kd = v % 3
             tile = jnp.where(lane < 96, tile, pltpu.roll(tiles[7 + v // 3], 96 - kd * 32, 1))
         g2s[:, :, v * 128:(v + 1) * 128] = (tile * scale_two).astype(BF16).reshape(tiles_n, rows_xy, 128)
-    pl.semaphore_wait(news.at[1], len(wide))
     for r in range(1, tiles_n):
         other, peer = xy_peer(r)
         send(g2s.at[other], g2x.at[xy], xs.at[0], xr.at[0], peer)

time: 33.9 us -> 33.9 us (level)
  no operation moved by 1% of the time
where the time goes in v7:
time: 33.9 us; the launch traced here: 33.8 us
  Pallas kernels  33.1 us (98%)
  between operations  0.64 us (2%)
    pallas_call x1, Pallas kernels, on_device(): pl.pallas_call(functools.partial(kernel, sizes, cols), out_shape=(jax.Sha...  32.4 us

profile of v7, /device:TPU:1, one launch (start us, length us, event | category | flops | bytes accessed | tf_op | source)
XLA Modules:
  0.0 33.8 jit_solution(5928893809658881755)
XLA Ops:
  0.6 32.4 %conv_step.1 = (bf16[64,2,256]{2,1,0:T(2,128)(2,1)S(1)}, bf16[32,2,256]{2,1,0:T(2,128)(2,1)S(1)}, f32[1,128]{1,0:T(1,128)S(1)}, f32[1,896]{1,0:T(1,128)S(1)}) custom-call(bf16[4,4,32,32]{3,2,1,0:T(8,128)(2,1)} %bitcast.11, bf16[27,4,32]{2,1,0:T(4,128)(2,1)} %bitcast.13, bf16[27,32,64]{2,1,0:T(8,128)(2,1)} %bitcast.10, bf16[64,2,256]{2,1,0:T(2,128)(2,1)} %bitcast.12), custom_call_target="tpu_custom_call" | custom-call | tf_op jit(solution)/shard_map/conv_step/pallas_call | solution.py:490
  33.1 0.7 %finish.1 = (bf16[64,2,256]{2,1,0:T(2,128)(2,1)}, bf16[32,2,256]{2,1,0:T(2,128)(2,1)}, f32[54]{0:T(128)}, f32[864]{0:T(1024)}) custom-call(bf16[64,2,256]{2,1,0:T(2,128)(2,1)S(1)} %get-tuple-element.12.feat, bf16[32,2,256]{2,1,0:T(2,128)(2,1)S(1)} %get-tuple-element.13.pgrad, f32[1,128]{1,0:T(1,128)S(1)} %get-tuple-element.14.g1, ...), custom_call_target="tpu_custom_call" | custom-call | tf_op jit(solution)/shard_map/finish/pallas_call | solution.py:515
